TPU v7x, 32 devices: a whole 2x2x4 slice. The times are simulated.
32 devices in a mesh: dp: 8 (over z, core), fsdp: 4 (over y, x).
Axes of the slice: x: 2, y: 2, z: 4, core: 2. Of those that a mesh axis runs over, the one named last changes fastest.
Arguments:
- tokens: bfloat16 [32768, 768], P(('dp', 'fsdp')), may hold values from -6 to 6
- segments: int32 [32768], P(('dp', 'fsdp')), may hold values from -1 to 15, as said below
- cotangent: bfloat16 [32768, 768], P(('dp', 'fsdp')), may hold values from -6 to 6
- qkv_weight: bfloat16 [768, 2304], P('fsdp'), may hold values from -0.21875 to 0.21875
- qkv_bias: bfloat16 [2304], P('fsdp'), may hold values from -1.796875 to 1.796875
- out_weight: bfloat16 [768, 768], P('fsdp'), may hold values from -0.875 to 0.875
- out_bias: bfloat16 [768], P('fsdp'), may hold values from -1.796875 to 1.796875
- up_weight: bfloat16 [768, 3072], P('fsdp'), may hold values from -0.21875 to 0.21875
- up_bias: bfloat16 [3072], P('fsdp'), may hold values from -1.796875 to 1.796875
- down_weight: bfloat16 [3072, 768], P('fsdp'), may hold values from -0.109375 to 0.109375
- down_bias: bfloat16 [768], P('fsdp'), may hold values from -1.796875 to 1.796875
- first_gain: bfloat16 [768], P('fsdp'), may hold values from 0.5 to 1.5
- first_shift: bfloat16 [768], P('fsdp'), may hold values from -1.796875 to 1.796875
- second_gain: bfloat16 [768], P('fsdp'), may hold values from 0.5 to 1.5
- second_shift: bfloat16 [768], P('fsdp'), may hold values from -1.796875 to 1.796875
- query_gain: bfloat16 [64], P('fsdp'), may hold values from 0.099609375 to 1.8984375
- key_gain: bfloat16 [64], P('fsdp'), may hold values from 0.099609375 to 1.8984375
Outputs:
- out_tokens: bfloat16 [32768, 768], P(('dp', 'fsdp'))
- tokens_grad: bfloat16 [32768, 768], P(('dp', 'fsdp'))
- qkv_weight_grad: float32 [768, 2304], P('fsdp')
- qkv_bias_grad: float32 [2304], P('fsdp')
- out_weight_grad: float32 [768, 768], P('fsdp')
- out_bias_grad: float32 [768], P('fsdp')
- up_weight_grad: float32 [768, 3072], P('fsdp')
- up_bias_grad: float32 [3072], P('fsdp')
- down_weight_grad: float32 [3072, 768], P('fsdp')
- down_bias_grad: float32 [768], P('fsdp')
- first_gain_grad: float32 [768], P('fsdp')
- first_shift_grad: float32 [768], P('fsdp')
- second_gain_grad: float32 [768], P('fsdp')
- second_shift_grad: float32 [768], P('fsdp')
- query_gain_grad: float32 [64], P('fsdp')
- key_gain_grad: float32 [64], P('fsdp')
Inputs may be any that keep to these rules, and one draw needn't show every extreme that they name: `segments`: within each device's block of 1024 patches, equal ids mark one image; -1 marks padding, whose output and gradient vanish. Half of all blocks hold 4 sequences of four small images of 64 patches each; the others hold one sequence: an image of 576 patches, a second image, then padding.
All inputs are finite; a program needn't handle non-finite values.
Results may differ from a plain program's by a relative error of at most 0.024.
Values may be sent and summed in bfloat16 or wider, within the bound.
A program may use at most 256 MiB of HBM per device.

v0:
```python
import jax
import jax.numpy as jnp
from jax import lax
from jax.sharding import PartitionSpec as P

norm_eps = 1e-06


def layer_norm(value, gain, shift):
    centred = value - jnp.mean(value, axis=-1, keepdims=True)
    scaled = centred * lax.rsqrt(jnp.mean(centred * centred, axis=-1, keepdims=True) + norm_eps)
    return scaled * gain + shift


def head_scale(value, gain):
    centred = value - jnp.mean(value, axis=-1, keepdims=True)
    return (
        centred * lax.rsqrt(jnp.mean(centred * centred, axis=-1, keepdims=True) + norm_eps) * gain
    )


def head_norms(query, keys, query_gain, key_gain):
    return (head_scale(query, query_gain), head_scale(keys, key_gain))


def exact_gelu(value):
    return jax.nn.gelu(value, approximate=False)


def left_product(left, right):
    return lax.dot_general(
        left, right, (((0,), (0,)), ((), ())), preferred_element_type=jnp.float32
    )


def right_product(left, right):
    return lax.dot_general(
        left, right, (((1,), (1,)), ((), ())), preferred_element_type=jnp.float32
    )


def block_scores(query_block, key_low, segment_block, segments):
    scores = (
        jnp.einsum("qhe,khe->hqk", query_block, key_low, preferred_element_type=jnp.float32) * 0.125
    )
    allowed = segment_block[:, None] == segments[None, :]
    return jnp.where(allowed[None], scores, -1e30)


def attend(query_low, key_low, value_low, segments):
    count = query_low.shape[0]
    block = min(512, count)

    def one_block(position):
        query_block = lax.dynamic_slice_in_dim(query_low, position * block, block, 0)
        segment_block = lax.dynamic_slice_in_dim(segments, position * block, block, 0)
        scores = block_scores(query_block, key_low, segment_block, segments)
        top = jnp.max(scores, axis=-1, keepdims=True)
        expo = jnp.exp(scores - top)
        total = jnp.sum(expo, axis=-1, keepdims=True)
        weights = (expo / total).astype(jnp.bfloat16)
        attended = jnp.einsum(
            "hqk,khe->qhe", weights, value_low, preferred_element_type=jnp.float32
        )
        return (attended, (top + jnp.log(total))[..., 0])

    attended, log_total = lax.map(one_block, jnp.arange(count // block, dtype=jnp.int32))
    return (attended.reshape(query_low.shape), log_total)


def attend_back(query_low, key_low, value_low, segments, grad_attended, log_total):
    count = query_low.shape[0]
    block = min(512, count)

    def one_block(carry, item):
        key_grad, value_grad = carry
        position, block_total = item
        query_block = lax.dynamic_slice_in_dim(query_low, position * block, block, 0)
        segment_block = lax.dynamic_slice_in_dim(segments, position * block, block, 0)
        grad_block = lax.dynamic_slice_in_dim(grad_attended, position * block, block, 0)
        scores = block_scores(query_block, key_low, segment_block, segments)
        weights = jnp.exp(scores - block_total[..., None])
        value_grad = value_grad + jnp.einsum(
            "hqk,qhe->khe",
            weights.astype(jnp.bfloat16),
            grad_block,
            preferred_element_type=jnp.float32,
        )
        grad_weights = jnp.einsum(
            "qhe,khe->hqk", grad_block, value_low, preferred_element_type=jnp.float32
        )
        grad_scores = weights * (
            grad_weights - jnp.sum(weights * grad_weights, axis=-1, keepdims=True)
        )
        scores_low = grad_scores.astype(jnp.bfloat16)
        query_grad = 0.125 * jnp.einsum(
            "hqk,khe->qhe", scores_low, key_low, preferred_element_type=jnp.float32
        )
        key_grad = key_grad + 0.125 * jnp.einsum(
            "hqk,qhe->khe", scores_low, query_block, preferred_element_type=jnp.float32
        )
        return ((key_grad, value_grad), query_grad)

    empty = jnp.zeros(key_low.shape, jnp.float32)
    (key_grad, value_grad), query_grad = lax.scan(
        one_block, (empty, empty), (jnp.arange(count // block, dtype=jnp.int32), log_total)
    )
    return (query_grad.reshape(query_low.shape), key_grad, value_grad)


def shards(
    tokens,
    segments,
    cotangent,
    qkv_weight,
    qkv_bias,
    out_weight,
    out_bias,
    up_weight,
    up_bias,
    down_weight,
    down_bias,
    first_gain,
    first_shift,
    second_gain,
    second_shift,
    query_gain,
    key_gain,
):
    gathered = (
        lax.all_gather(qkv_weight, "fsdp", axis=0, tiled=True),
        lax.all_gather(qkv_bias, "fsdp", axis=0, tiled=True),
        lax.all_gather(out_weight, "fsdp", axis=0, tiled=True),
        lax.all_gather(out_bias, "fsdp", axis=0, tiled=True),
        lax.all_gather(up_weight, "fsdp", axis=0, tiled=True),
        lax.all_gather(up_bias, "fsdp", axis=0, tiled=True),
        lax.all_gather(down_weight, "fsdp", axis=0, tiled=True),
        lax.all_gather(down_bias, "fsdp", axis=0, tiled=True),
        lax.all_gather(first_gain, "fsdp", axis=0, tiled=True),
        lax.all_gather(first_shift, "fsdp", axis=0, tiled=True),
        lax.all_gather(second_gain, "fsdp", axis=0, tiled=True),
        lax.all_gather(second_shift, "fsdp", axis=0, tiled=True),
        lax.all_gather(query_gain, "fsdp", axis=0, tiled=True),
        lax.all_gather(key_gain, "fsdp", axis=0, tiled=True),
    )
    (
        qkv_matrix,
        qkv_offset,
        proj_matrix,
        proj_offset,
        up_matrix,
        up_offset,
        down_matrix,
        down_offset,
        gain_first,
        shift_first,
        gain_second,
        shift_second,
        gain_query,
        gain_key,
    ) = gathered
    count = tokens.shape[0]
    width = tokens.shape[1]
    head_size = gain_query.shape[0]
    heads = width // head_size
    float_tokens = tokens.astype(jnp.float32)
    normed_first, first_back = jax.vjp(
        layer_norm, float_tokens, gain_first.astype(jnp.float32), shift_first.astype(jnp.float32)
    )
    normed_low = normed_first.astype(jnp.bfloat16)
    mixed = jnp.dot(normed_low, qkv_matrix, preferred_element_type=jnp.float32) + qkv_offset.astype(
        jnp.float32
    )
    query = mixed[:, :width].reshape(count, heads, head_size)
    keys = mixed[:, width : 2 * width].reshape(count, heads, head_size)
    value_low = mixed[:, 2 * width :].reshape(count, heads, head_size).astype(jnp.bfloat16)
    (query_norm, key_norm), norm_back = jax.vjp(
        head_norms, query, keys, gain_query.astype(jnp.float32), gain_key.astype(jnp.float32)
    )
    query_low = query_norm.astype(jnp.bfloat16)
    key_low = key_norm.astype(jnp.bfloat16)
    attended, log_total = attend(query_low, key_low, value_low, segments)
    attended_low = attended.reshape(count, width).astype(jnp.bfloat16)
    residual = (
        float_tokens
        + jnp.dot(attended_low, proj_matrix, preferred_element_type=jnp.float32)
        + proj_offset.astype(jnp.float32)
    )
    normed_second, second_back = jax.vjp(
        layer_norm, residual, gain_second.astype(jnp.float32), shift_second.astype(jnp.float32)
    )
    second_low = normed_second.astype(jnp.bfloat16)
    hidden = jnp.dot(second_low, up_matrix, preferred_element_type=jnp.float32) + up_offset.astype(
        jnp.float32
    )
    active, gelu_back = jax.vjp(exact_gelu, hidden)
    active_low = active.astype(jnp.bfloat16)
    result = jnp.dot(
        active_low, down_matrix, preferred_element_type=jnp.float32
    ) + down_offset.astype(jnp.float32)
    valid = (segments >= 0)[:, None]
    output = jnp.where(valid, residual + result, 0.0).astype(jnp.bfloat16)
    weights_back = (
        lax.all_gather(qkv_weight, "fsdp", axis=0, tiled=True),
        lax.all_gather(qkv_bias, "fsdp", axis=0, tiled=True),
        lax.all_gather(out_weight, "fsdp", axis=0, tiled=True),
        lax.all_gather(out_bias, "fsdp", axis=0, tiled=True),
        lax.all_gather(up_weight, "fsdp", axis=0, tiled=True),
        lax.all_gather(up_bias, "fsdp", axis=0, tiled=True),
        lax.all_gather(down_weight, "fsdp", axis=0, tiled=True),
        lax.all_gather(down_bias, "fsdp", axis=0, tiled=True),
        lax.all_gather(first_gain, "fsdp", axis=0, tiled=True),
        lax.all_gather(first_shift, "fsdp", axis=0, tiled=True),
        lax.all_gather(second_gain, "fsdp", axis=0, tiled=True),
        lax.all_gather(second_shift, "fsdp", axis=0, tiled=True),
        lax.all_gather(query_gain, "fsdp", axis=0, tiled=True),
        lax.all_gather(key_gain, "fsdp", axis=0, tiled=True),
    )
    qkv_again = weights_back[0]
    proj_again = weights_back[2]
    up_again = weights_back[4]
    down_again = weights_back[6]
    grad_output = jnp.where(valid, cotangent.astype(jnp.float32), 0.0)
    result_low = grad_output.astype(jnp.bfloat16)
    down_grad = left_product(active_low, result_low)
    down_offset_grad = jnp.sum(result_low.astype(jnp.float32), axis=0)
    (grad_hidden,) = gelu_back(right_product(result_low, down_again))
    hidden_low = grad_hidden.astype(jnp.bfloat16)
    up_grad = left_product(second_low, hidden_low)
    up_offset_grad = jnp.sum(hidden_low.astype(jnp.float32), axis=0)
    grad_norm_second, second_gain_grad, second_shift_grad = second_back(
        right_product(hidden_low, up_again)
    )
    grad_residual = grad_output + grad_norm_second
    branch_low = grad_residual.astype(jnp.bfloat16)
    proj_grad = left_product(attended_low, branch_low)
    proj_offset_grad = jnp.sum(branch_low.astype(jnp.float32), axis=0)
    grad_attended = (
        right_product(branch_low, proj_again).astype(jnp.bfloat16).reshape(count, heads, head_size)
    )
    query_grad, key_grad, value_grad = attend_back(
        query_low, key_low, value_low, segments, grad_attended, log_total
    )
    grad_query, grad_keys, query_gain_grad, key_gain_grad = norm_back((query_grad, key_grad))
    grad_mixed = jnp.concatenate(
        [
            grad_query.reshape(count, width),
            grad_keys.reshape(count, width),
            value_grad.reshape(count, width),
        ],
        axis=1,
    ).astype(jnp.bfloat16)
    qkv_grad = left_product(normed_low, grad_mixed)
    qkv_offset_grad = jnp.sum(grad_mixed.astype(jnp.float32), axis=0)
    grad_norm_first, first_gain_grad, first_shift_grad = first_back(
        right_product(grad_mixed, qkv_again)
    )
    grad_input = (grad_residual + grad_norm_first).astype(jnp.bfloat16)
    summed = (
        lax.psum_scatter(
            qkv_grad.astype(jnp.bfloat16), "fsdp", scatter_dimension=0, tiled=True
        ).astype(jnp.float32),
        lax.psum_scatter(
            qkv_offset_grad.astype(jnp.bfloat16), "fsdp", scatter_dimension=0, tiled=True
        ).astype(jnp.float32),
        lax.psum_scatter(
            proj_grad.astype(jnp.bfloat16), "fsdp", scatter_dimension=0, tiled=True
        ).astype(jnp.float32),
        lax.psum_scatter(
            proj_offset_grad.astype(jnp.bfloat16), "fsdp", scatter_dimension=0, tiled=True
        ).astype(jnp.float32),
        lax.psum_scatter(
            up_grad.astype(jnp.bfloat16), "fsdp", scatter_dimension=0, tiled=True
        ).astype(jnp.float32),
        lax.psum_scatter(
            up_offset_grad.astype(jnp.bfloat16), "fsdp", scatter_dimension=0, tiled=True
        ).astype(jnp.float32),
        lax.psum_scatter(
            down_grad.astype(jnp.bfloat16), "fsdp", scatter_dimension=0, tiled=True
        ).astype(jnp.float32),
        lax.psum_scatter(
            down_offset_grad.astype(jnp.bfloat16), "fsdp", scatter_dimension=0, tiled=True
        ).astype(jnp.float32),
        lax.psum_scatter(
            first_gain_grad.astype(jnp.bfloat16), "fsdp", scatter_dimension=0, tiled=True
        ).astype(jnp.float32),
        lax.psum_scatter(
            first_shift_grad.astype(jnp.bfloat16), "fsdp", scatter_dimension=0, tiled=True
        ).astype(jnp.float32),
        lax.psum_scatter(
            second_gain_grad.astype(jnp.bfloat16), "fsdp", scatter_dimension=0, tiled=True
        ).astype(jnp.float32),
        lax.psum_scatter(
            second_shift_grad.astype(jnp.bfloat16), "fsdp", scatter_dimension=0, tiled=True
        ).astype(jnp.float32),
        lax.psum_scatter(
            query_gain_grad.astype(jnp.bfloat16), "fsdp", scatter_dimension=0, tiled=True
        ).astype(jnp.float32),
        lax.psum_scatter(
            key_gain_grad.astype(jnp.bfloat16), "fsdp", scatter_dimension=0, tiled=True
        ).astype(jnp.float32),
    )
    final = (
        lax.psum(summed[0].astype(jnp.bfloat16), "dp").astype(jnp.float32),
        lax.psum(summed[1].astype(jnp.bfloat16), "dp").astype(jnp.float32),
        lax.psum(summed[2].astype(jnp.bfloat16), "dp").astype(jnp.float32),
        lax.psum(summed[3].astype(jnp.bfloat16), "dp").astype(jnp.float32),
        lax.psum(summed[4].astype(jnp.bfloat16), "dp").astype(jnp.float32),
        lax.psum(summed[5].astype(jnp.bfloat16), "dp").astype(jnp.float32),
        lax.psum(summed[6].astype(jnp.bfloat16), "dp").astype(jnp.float32),
        lax.psum(summed[7].astype(jnp.bfloat16), "dp").astype(jnp.float32),
        lax.psum(summed[8].astype(jnp.bfloat16), "dp").astype(jnp.float32),
        lax.psum(summed[9].astype(jnp.bfloat16), "dp").astype(jnp.float32),
        lax.psum(summed[10].astype(jnp.bfloat16), "dp").astype(jnp.float32),
        lax.psum(summed[11].astype(jnp.bfloat16), "dp").astype(jnp.float32),
        lax.psum(summed[12].astype(jnp.bfloat16), "dp").astype(jnp.float32),
        lax.psum(summed[13].astype(jnp.bfloat16), "dp").astype(jnp.float32),
    )
    return (
        output,
        grad_input,
        final[0],
        final[1],
        final[2],
        final[3],
        final[4],
        final[5],
        final[6],
        final[7],
        final[8],
        final[9],
        final[10],
        final[11],
        final[12],
        final[13],
    )


def solution(mesh):
    in_specs = (
        P(("dp", "fsdp"), None),
        P(("dp", "fsdp")),
        P(("dp", "fsdp"), None),
        P("fsdp", None),
        P("fsdp"),
        P("fsdp", None),
        P("fsdp"),
        P("fsdp", None),
        P("fsdp"),
        P("fsdp", None),
        P("fsdp"),
        P("fsdp"),
        P("fsdp"),
        P("fsdp"),
        P("fsdp"),
        P("fsdp"),
        P("fsdp"),
    )
    out_specs = (
        P(("dp", "fsdp"), None),
        P(("dp", "fsdp"), None),
        P("fsdp", None),
        P("fsdp"),
        P("fsdp", None),
        P("fsdp"),
        P("fsdp", None),
        P("fsdp"),
        P("fsdp", None),
        P("fsdp"),
        P("fsdp"),
        P("fsdp"),
        P("fsdp"),
        P("fsdp"),
        P("fsdp"),
        P("fsdp"),
    )
    return jax.shard_map(shards, mesh=mesh, in_specs=in_specs, out_specs=out_specs, check_vma=False)
```

profile of v0, /device:TPU:0, one launch (start us, length us, event | category | flops | bytes accessed | tf_op | source)
XLA Modules:
  0.0 847.7 jit_solution(16748366694479090211)
XLA Ops:
  14.7 19.0 %all-reduce.22 = (bf16[2304]{0:T(1024)(128)(2,1)S(1)}, bf16[768]{0:T(1024)(128)(2,1)S(1)}, bf16[768]{0:T(1024)(128)(2,1)S(1)}, bf16[64]{0:T(256)(128)(2,1)S(1)},...) all-reduce(bf16[2304]{0:T(1024)(128)(2,1)S(1)} %dynamic-update-slic, ...), channel_id=1, replica_groups=mesh['dp'=8,'fsdp'=4] {'fsdp'}, use_global_device_ids=true, to_apply=%add.2 | all-reduce | flops 6272 | bytes 25088
  37.2 7.8 all-gather
  48.5 11.7 %all-gather.6.cloned.1.call-done = bf16[768,2304]{1,0:T(8,128)(2,1)} async-done(((bf16[192,2304]{1,0:T(8,128)(2,1)}), bf16[768,2304]{1,0:T(8,128)(2,1)}) %all-gather.6.cloned.1.call-update) | async-done | bytes 3538960 | tf_op jit(solution)/shard_map/all_gather | solution.py:131
  60.1 6.3 convolution_add_fusion
  88.5 4.1 multiply_convert_fusion.2
  92.6 74.7 %while.27 = (s32[]{:T(128)}, bf16[2,512,12,64]{1,3,2,0:T(8,128)(2,1)}, f32[2,12,512]{2,1,0:T(8,128)S(1)}, s32[2]{0:T(128)S(1)}, s32[1024]{0:T(1024)S(1)}, /*inde...) while((s32[]{:T(128)}, ...), condition=%wide.region_9.10_spmd, body=%wide.region_6.9_spmd.sunk | while | flops 1686628352 | bytes 190286576 | solution.py:67
  94.6 11.5 %fusion.114 = (f32[12,512]{1,0:T(8,128)S(1)}, f32[12,512,1024]{2,1,0:T(8,128)}) fusion(pred[512,1024]{1,0:T(8,128)(4,1)S(1)} %broadcast_compare_fusion.5, bf16[1024,12,64]{0,2,1:T(8,128)(2,1)S(1)} %get-tuple-element.489, bf16[1024,12,64]{0,2,1:T(8,128)(2,1)S(1)} %get-tuple-element.488, s32[]{:T(128)S(6)} %select_n.77), kind=kOutput, calls=%fused_computation.3.clone.1 | convolution fusion | flops 824174592 | bytes 28073988 | tf_op jit(solution)/shard_map/while/body/eval_jaxpr/qhe,khe->hqk/dot_general | solution.py:44
  106.1 12.3 %fusion.115 = f32[12,512]{1,0:T(8,128)S(1)} fusion(f32[12,512,1024]{2,1,0:T(8,128)} %get-tuple-element.444, f32[12,512]{1,0:T(8,128)S(1)} %get-tuple-element.445, pred[512,1024]{1,0:T(8,128)(4,1)S(1)} %broadcast_compare_fusion.5), kind=kLoop, calls=%fused_computation.4.clone.1 | loop fusion | flops 25159680 | bytes 25739264 | tf_op jit(solution)/shard_map/while/body/eval_jaxpr/reduce_sum | solution.py:60
  121.9 8.5 %bitcast_dynamic-update-slice_fusion.4 = bf16[2,512,12,64]{1,3,2,0:T(8,128)(2,1)} fusion(bf16[2,512,12,64]{1,3,2,0:T(8,128)(2,1)} %get-tuple-element.472, s32[]{:T(128)} %get-tuple-element.471, bf16[1024,12,64]{0,2,1:T(8,128)(2,1)S(1)} %copy-done.10, f32[12,512,1024]{2,1,0:T(8,128)S(1)} %copy-done, f32[12,512]{1,0:T(8,128)S(1)} %fusion.115, ...), kind=kOutput, calls=%fused_computation.6.clone.1 | convolution fusion | flops 836763648 | bytes 28885504 | tf_op jit(solution)/shard_map/while/body/eval_jaxpr/hqk,khe->qhe/dot_general | solution.py:62
  132.1 10.7 %fusion.114 = (f32[12,512]{1,0:T(8,128)S(1)}, f32[12,512,1024]{2,1,0:T(8,128)}) fusion(pred[512,1024]{1,0:T(8,128)(4,1)S(1)} %broadcast_compare_fusion.5, bf16[1024,12,64]{0,2,1:T(8,128)(2,1)S(1)} %get-tuple-element.489, bf16[1024,12,64]{0,2,1:T(8,128)(2,1)S(1)} %get-tuple-element.488, s32[]{:T(128)S(6)} %select_n.77), kind=kOutput, calls=%fused_computation.3.clone.1 | convolution fusion | flops 824174592 | bytes 28073988 | tf_op jit(solution)/shard_map/while/body/eval_jaxpr/qhe,khe->hqk/dot_general | solution.py:44
  142.7 12.3 %fusion.115 = f32[12,512]{1,0:T(8,128)S(1)} fusion(f32[12,512,1024]{2,1,0:T(8,128)} %get-tuple-element.444, f32[12,512]{1,0:T(8,128)S(1)} %get-tuple-element.445, pred[512,1024]{1,0:T(8,128)(4,1)S(1)} %broadcast_compare_fusion.5), kind=kLoop, calls=%fused_computation.4.clone.1 | loop fusion | flops 25159680 | bytes 25739264 | tf_op jit(solution)/shard_map/while/body/eval_jaxpr/reduce_sum | solution.py:60
  158.8 8.5 %bitcast_dynamic-update-slice_fusion.4 = bf16[2,512,12,64]{1,3,2,0:T(8,128)(2,1)} fusion(bf16[2,512,12,64]{1,3,2,0:T(8,128)(2,1)} %get-tuple-element.472, s32[]{:T(128)} %get-tuple-element.471, bf16[1024,12,64]{0,2,1:T(8,128)(2,1)S(1)} %copy-done.10, f32[12,512,1024]{2,1,0:T(8,128)S(1)} %copy-done, f32[12,512]{1,0:T(8,128)S(1)} %fusion.115, ...), kind=kOutput, calls=%fused_computation.6.clone.1 | convolution fusion | flops 836763648 | bytes 28885504 | tf_op jit(solution)/shard_map/while/body/eval_jaxpr/hqk,khe->qhe/dot_general | solution.py:62
  178.8 4.3 copy.88
  188.7 38.1 %multiply_convert_fusion.1 = (bf16[1024,3072]{1,0:T(8,128)(2,1)}, f32[1024,3072]{1,0:T(8,128)}, f32[1024,3072]{1,0:T(8,128)}) fusion(f32[3072]{0:T(1024)S(1)} %bitcast.137, bf16[768,3072]{1,0:T(8,128)(2,1)} %all-gather.10.cloned.1.call-done, f32[1024,768]{0,1:T(8,128)} %copy-done.14, f32[768]{0:T(1024)S(1)} %copy-done.81, f32[768]{0:T(1024)S(1)} %copy-done.63, ...), kind=kOutput, calls=%fused_computation.40 | convolution fusion | flops 5043388416 | bytes 39348224 | tf_op jit(solution)/shard_map/dot_general | solution.py:193
  226.9 19.2 %fusion.72 = (bf16[3072]{0:T(1024)(128)(2,1)}, bf16[1024,3072]{1,0:T(8,128)(2,1)}) fusion(f32[1024,3072]{1,0:T(8,128)} %get-tuple-element.310, bf16[3072,768]{1,0:T(8,128)(2,1)} %all-gather.12.cloned.1.call-done, bf16[1024,768]{0,1:T(8,128)(2,1)} %copy.84, pred[1024]{0:T(1024)(128)(4,1)S(1)} %copy-done.69, f32[1024,3072]{1,0:T(8,128)} %get-tuple-element.326, ...), kind=kOutput, calls=%fused_computation.139 | convolution fusion | flops 4884526080 | bytes 37768192 | tf_op jit(solution)/shard_map/dot_general | solution.py:37
  246.1 10.3 %fusion.74 = (bf16[768]{0:T(1024)(128)(2,1)}, f32[1024,768]{1,0:T(8,128)}) fusion(bf16[1024,3072]{1,0:T(8,128)(2,1)} %get-tuple-element.328, bf16[768,3072]{1,0:T(8,128)(2,1)} %all-gather.10.cloned.1.call-done), kind=kOutput, calls=%fused_computation.141 | convolution fusion | flops 4832623616 | bytes 14157312 | tf_op jit(solution)/shard_map/dot_general | solution.py:37
  259.9 4.5 multiply_reduce_fusion.3
  270.3 232.9 %while.28 = (s32[]{:T(128)}, f32[1024,12,64]{0,2,1:T(8,128)}, f32[1024,12,64]{0,2,1:T(8,128)}, f32[2,512,12,64]{1,0,3,2:T(2,128)}, s32[2]{0:T(128)S(1)}, /*index...) while((s32[]{:T(128)}, f32[1024,12,64]{0,2,1:T(8,128)}, ...), condition=%wide.region_16.17_spmd.clone, body=%wide.region_14.16_spmd.clone.sunk | while | flops 4125747200 | bytes 242411920 | solution.py:105
  272.1 10.1 %fusion.125 = f32[12,512,1024]{2,1,0:T(8,128)} fusion(bf16[1024,12,64]{0,2,1:T(8,128)(2,1)S(1)} %get-tuple-element.532, bf16[1024,12,64]{0,2,1:T(8,128)(2,1)S(1)} %get-tuple-element.530, s32[]{:T(128)S(6)} %select_n.81), kind=kOutput, calls=%fused_computation.28.clone.1 | convolution fusion | flops 805306368 | bytes 27525124 | tf_op jit(solution)/shard_map/while/body/eval_jaxpr/qhe,khe->hqk/dot_general | solution.py:44
  282.7 18.3 %multiply_reduce_fusion.11 = (f32[12,512]{1,0:T(8,128)S(1)}, f32[12,512,1024]{2,1,0:T(8,128)}) fusion(f32[12,512,1024]{2,1,0:T(8,128)} %fusion.125, f32[12,512]{1,0:T(8,128)S(1)} %dynamic-slice_bitcast_fusion.2, pred[512,1024]{1,0:T(8,128)(4,1)S(1)} %broadcast_compare_fusion.6, bf16[1024,12,64]{0,2,1:T(8,128)(2,1)} %get-tuple-element.535, ...), kind=kOutput, calls=%fused_computation.15.clone.1 | convolution fusion | flops 836757504 | bytes 53264388 | tf_op jit(solution)/shard_map/while/body/eval_jaxpr/qhe,khe->hqk/dot_general | solution.py:89
  300.9 21.2 %multiply_convert_fusion.5 = bf16[12,512,1024]{2,1,0:T(8,128)(2,1)} fusion(f32[12,512,1024]{2,1,0:T(8,128)} %get-tuple-element.457, f32[12,512,1024]{2,1,0:T(8,128)} %fusion.125, f32[12,512]{1,0:T(8,128)S(1)} %get-tuple-element.458, f32[12,512]{1,0:T(8,128)S(1)} %dynamic-slice_bitcast_fusion.2, pred[512,1024]{1,0:T(8,128)(4,1)S(1)} %broadcast_compare_fusion.6), kind=kLoop, calls=%fused_computation.14.clone.1 | loop fusion | flops 37748736 | bytes 63488000 | tf_op jit(solution)/shard_map/while/body/eval_jaxpr/convert_element_type | solution.py:95
  322.2 9.7 %multiply_bitcast_fusion.3 = f32[1,512,12,64]{1,3,2,0:T(8,128)} fusion(bf16[12,512,1024]{2,1,0:T(8,128)(2,1)} %multiply_convert_fusion.5, bf16[1024,12,64]{0,2,1:T(8,128)(2,1)S(1)} %get-tuple-element.532), kind=kOutput, calls=%fused_computation.22.clone.1 | convolution fusion | flops 805699584 | bytes 15728640 | tf_op jit(solution)/shard_map/while/body/eval_jaxpr/hqk,khe->qhe/dot_general | solution.py:96
  334.9 28.8 %dynamic_update_slice.19 = f32[2,512,12,64]{1,0,3,2:T(2,128)} dynamic-update-slice(f32[2,512,12,64]{1,0,3,2:T(2,128)} %get-tuple-element.513, f32[1,512,12,64]{1,0,3,2:T(1,128)S(1)} %copy.132, s32[]{:T(128)} %get-tuple-element.510, s32[]{:T(128)} %constant.71.clone.1..sunk.1, s32[]{:T(128)} %constant.71.clone.1..sunk.1, s32[]{:T(128)} %constant.71.clone.1..sunk.1) | dynamic-update-slice | bytes 3145732 | tf_op jit(solution)/shard_map/while/body/jit(dynamic_update_index_in_dim)/dynamic_update_slice | solution.py:67
  363.7 8.9 %bitcast_add_fusion.4 = f32[1024,12,64]{0,2,1:T(8,128)} fusion(f32[1024,12,64]{0,2,1:T(8,128)} %get-tuple-element.511, bf16[12,512,1024]{2,1,0:T(8,128)(2,1)} %multiply_convert_fusion.5, pred[]{:T(512)S(6)} %compare.3, bf16[1024,12,64]{0,2,1:T(8,128)(2,1)} %copy-done.6, s32[]{:T(128)S(6)} %select_n.81), kind=kOutput, calls=%fused_computation.21.clone.1 | convolution fusion | flops 807665664 | bytes 19660804 | tf_op jit(solution)/shard_map/while/body/eval_jaxpr/hqk,qhe->khe/dot_general | solution.py:99
  372.6 13.4 %bitcast_add_fusion.5 = f32[1024,12,64]{0,2,1:T(8,128)} fusion(f32[1024,12,64]{0,2,1:T(8,128)} %get-tuple-element.512, f32[12,512,1024]{2,1,0:T(8,128)} %fusion.125, f32[12,512]{1,0:T(8,128)S(1)} %dynamic-slice_bitcast_fusion.2, pred[512,1024]{1,0:T(8,128)(4,1)S(1)} %copy-done.5, pred[]{:T(512)S(6)} %compare.3, ...), kind=kOutput, calls=%fused_computation.20.clone.1 | convolution fusion | flops 832045056 | bytes 32800772 | tf_op jit(solution)/shard_map/while/body/eval_jaxpr/hqk,qhe->khe/dot_general | solution.py:83
  387.3 10.1 %fusion.125 = f32[12,512,1024]{2,1,0:T(8,128)} fusion(bf16[1024,12,64]{0,2,1:T(8,128)(2,1)S(1)} %get-tuple-element.532, bf16[1024,12,64]{0,2,1:T(8,128)(2,1)S(1)} %get-tuple-element.530, s32[]{:T(128)S(6)} %select_n.81), kind=kOutput, calls=%fused_computation.28.clone.1 | convolution fusion | flops 805306368 | bytes 27525124 | tf_op jit(solution)/shard_map/while/body/eval_jaxpr/qhe,khe->hqk/dot_general | solution.py:44
  398.0 18.3 %multiply_reduce_fusion.11 = (f32[12,512]{1,0:T(8,128)S(1)}, f32[12,512,1024]{2,1,0:T(8,128)}) fusion(f32[12,512,1024]{2,1,0:T(8,128)} %fusion.125, f32[12,512]{1,0:T(8,128)S(1)} %dynamic-slice_bitcast_fusion.2, pred[512,1024]{1,0:T(8,128)(4,1)S(1)} %broadcast_compare_fusion.6, bf16[1024,12,64]{0,2,1:T(8,128)(2,1)} %get-tuple-element.535, ...), kind=kOutput, calls=%fused_computation.15.clone.1 | convolution fusion | flops 836757504 | bytes 53264388 | tf_op jit(solution)/shard_map/while/body/eval_jaxpr/qhe,khe->hqk/dot_general | solution.py:89
  416.2 21.2 %multiply_convert_fusion.5 = bf16[12,512,1024]{2,1,0:T(8,128)(2,1)} fusion(f32[12,512,1024]{2,1,0:T(8,128)} %get-tuple-element.457, f32[12,512,1024]{2,1,0:T(8,128)} %fusion.125, f32[12,512]{1,0:T(8,128)S(1)} %get-tuple-element.458, f32[12,512]{1,0:T(8,128)S(1)} %dynamic-slice_bitcast_fusion.2, pred[512,1024]{1,0:T(8,128)(4,1)S(1)} %broadcast_compare_fusion.6), kind=kLoop, calls=%fused_computation.14.clone.1 | loop fusion | flops 37748736 | bytes 63488000 | tf_op jit(solution)/shard_map/while/body/eval_jaxpr/convert_element_type | solution.py:95
  437.4 9.7 %multiply_bitcast_fusion.3 = f32[1,512,12,64]{1,3,2,0:T(8,128)} fusion(bf16[12,512,1024]{2,1,0:T(8,128)(2,1)} %multiply_convert_fusion.5, bf16[1024,12,64]{0,2,1:T(8,128)(2,1)S(1)} %get-tuple-element.532), kind=kOutput, calls=%fused_computation.22.clone.1 | convolution fusion | flops 805699584 | bytes 15728640 | tf_op jit(solution)/shard_map/while/body/eval_jaxpr/hqk,khe->qhe/dot_general | solution.py:96
  450.1 28.8 %dynamic_update_slice.19 = f32[2,512,12,64]{1,0,3,2:T(2,128)} dynamic-update-slice(f32[2,512,12,64]{1,0,3,2:T(2,128)} %get-tuple-element.513, f32[1,512,12,64]{1,0,3,2:T(1,128)S(1)} %copy.132, s32[]{:T(128)} %get-tuple-element.510, s32[]{:T(128)} %constant.71.clone.1..sunk.1, s32[]{:T(128)} %constant.71.clone.1..sunk.1, s32[]{:T(128)} %constant.71.clone.1..sunk.1) | dynamic-update-slice | bytes 3145732 | tf_op jit(solution)/shard_map/while/body/jit(dynamic_update_index_in_dim)/dynamic_update_slice | solution.py:67
  478.9 9.8 %bitcast_add_fusion.4 = f32[1024,12,64]{0,2,1:T(8,128)} fusion(f32[1024,12,64]{0,2,1:T(8,128)} %get-tuple-element.511, bf16[12,512,1024]{2,1,0:T(8,128)(2,1)} %multiply_convert_fusion.5, pred[]{:T(512)S(6)} %compare.3, bf16[1024,12,64]{0,2,1:T(8,128)(2,1)} %copy-done.6, s32[]{:T(128)S(6)} %select_n.81), kind=kOutput, calls=%fused_computation.21.clone.1 | convolution fusion | flops 807665664 | bytes 19660804 | tf_op jit(solution)/shard_map/while/body/eval_jaxpr/hqk,qhe->khe/dot_general | solution.py:99
  488.7 14.3 %bitcast_add_fusion.5 = f32[1024,12,64]{0,2,1:T(8,128)} fusion(f32[1024,12,64]{0,2,1:T(8,128)} %get-tuple-element.512, f32[12,512,1024]{2,1,0:T(8,128)} %fusion.125, f32[12,512]{1,0:T(8,128)S(1)} %dynamic-slice_bitcast_fusion.2, pred[512,1024]{1,0:T(8,128)(4,1)S(1)} %copy-done.5, pred[]{:T(512)S(6)} %compare.3, ...), kind=kOutput, calls=%fused_computation.20.clone.1 | convolution fusion | flops 832045056 | bytes 32800772 | tf_op jit(solution)/shard_map/while/body/eval_jaxpr/hqk,qhe->khe/dot_general | solution.py:83
  503.2 5.8 reshape.304
  512.0 4.5 convolution_convert_fusion.4
  516.7 10.2 %multiply_reduce_fusion.2 = (bf16[64]{0:T(256)(128)(2,1)S(1)}, f32[2,512,12]{1,0,2:T(2,128)S(1)}) fusion(f32[2,512,12,64]{1,0,3,2:T(2,128)S(1)} %copy-done.17, f32[2,512,12,64]{1,0,3,2:T(2,128)} %reshape.305, f32[2,512,12]{1,0,2:T(2,128)S(1)} %copy-done.50, f32[2,512,12]{1,0,2:T(2,128)S(1)} %get-tuple-element.321, f32[2,512,12]{1,0,2:T(2,128)S(1)} %get-tuple-element.320, ...), kind=kLoop, calls=%fused_computation.84 | loop fusion | flops 7851968 | bytes 6488448 | tf_op jit(solution)/shard_map/transpose(jvp())/reduce_sum | solution.py:18
  549.2 4.0 add_convert_fusion.2
  559.4 8.1 fusion.45
  568.7 5.9 convolution_convert_fusion.2
  575.4 9.9 %convolution_convert_fusion.1 = bf16[768,3072]{1,0:T(8,128)(2,1)} fusion(bf16[1024,3072]{1,0:T(8,128)(2,1)} %get-tuple-element.328, f32[1024,768]{0,1:T(8,128)} %copy-done.14, f32[768]{0:T(1024)S(1)} %copy-done.82, f32[768]{0:T(1024)S(1)} %copy-done.64, f32[1024]{0:T(1024)S(1)} %copy-done.66, f32[1024]{0:T(1024)S(1)} %copy-done.56), kind=kOutput, calls=%fused_computation.56 | convolution fusion | flops 4838129664 | bytes 14170112 | tf_op jit(solution)/shard_map/dot_general | solution.py:31
  587.1 9.8 %convolution_convert_fusion = bf16[3072,768]{1,0:T(8,128)(2,1)} fusion(bf16[1024,3072]{1,0:T(8,128)(2,1)} %get-tuple-element.309, bf16[1024,768]{0,1:T(8,128)(2,1)S(1)} %copy-done.21, pred[1024]{0:T(1024)(128)(4,1)S(1)} %copy-done.70), kind=kOutput, calls=%fused_computation.55 | convolution fusion | flops 4836556800 | bytes 12583936 | tf_op jit(solution)/shard_map/dot_general | solution.py:31
  600.1 9.0 %fusion.73 = (bf16[768]{0:T(1024)(128)(2,1)S(1)}, f32[1024,768]{1,0:T(8,128)}) fusion(bf16[768,2304]{1,0:T(8,128)(2,1)} %all-gather.6.cloned.1.call-done, bf16[1024,768]{1,0:T(8,128)(2,1)} %copy.96, bf16[1024,768]{1,0:T(8,128)(2,1)} %copy-done.24, bf16[1024,768]{1,0:T(8,128)(2,1)} %copy-done.28), kind=kOutput, calls=%fused_computation.140 | convolution fusion | flops 3638820096 | bytes 11404800 | tf_op jit(solution)/shard_map/dot_general | solution.py:37
  619.3 14.8 %all-reduce.21 = (bf16[768]{0:T(1024)(128)(2,1)S(1)}, bf16[2304]{0:T(1024)(128)(2,1)S(1)}, bf16[768]{0:T(1024)(128)(2,1)S(1)}, bf16[3072]{0:T(1024)(128)(2,1)S(1...) all-reduce(bf16[768]{0:T(1024)(128)(2,1)S(1)} %dynamic-update-slice, ...), channel_id=1, replica_groups=mesh['dp'=8,'fsdp'=4] {'fsdp'}, use_global_device_ids=true, to_apply=%add.8 | all-reduce | flops 10880 | bytes 43520
  634.8 13.9 %all-reduce.19 = (bf16[576]{0:T(1024)(128)(2,1)S(1)}, bf16[192]{0:T(256)(128)(2,1)S(1)}, bf16[768]{0:T(1024)(128)(2,1)S(1)}, bf16[192]{0:T(256)(128)(2,1)S(1)}, ...) all-reduce(bf16[576]{0:T(1024)(128)(2,1)S(1)} %dynamic-slice.10, ...), channel_id=1, replica_groups=mesh['dp'=8,'fsdp'=4] {'dp'}, use_global_device_ids=true, to_apply=%region_27.28 | all-reduce | flops 2528 | bytes 10112 | tf_op jit(solution)/shard_map/psum | solution.py:305
  654.3 5.6 add_convert_fusion.1
  662.7 24.3 %reduce-scatter.9.cloned.1.call-done = bf16[192,3072]{1,0:T(8,128)(2,1)} async-done(((bf16[768,3072]{1,0:T(8,128)(2,1)}), bf16[192,3072]{1,0:T(8,128)(2,1)}) %reduce-scatter.9.cloned.1.call-update) | async-done | bytes 1179664 | tf_op jit(solution)/shard_map/reduce_scatter | solution.py:272
  687.0 60.0 %reduce-scatter.11.cloned.1.call-done = bf16[768,768]{1,0:T(8,128)(2,1)} async-done(((bf16[3072,768]{1,0:T(8,128)(2,1)}), bf16[768,768]{1,0:T(8,128)(2,1)}) %reduce-scatter.11.cloned.1.call-update) | async-done | bytes 1179664 | tf_op jit(solution)/shard_map/reduce_scatter | solution.py:278
  747.0 9.5 %select_convert_fusion = bf16[1024,768]{0,1:T(8,128)(2,1)} fusion(f32[1024,768]{0,1:T(8,128)S(1)} %copy-done.16, bf16[1024,3072]{1,0:T(8,128)(2,1)} %get-tuple-element.309, bf16[3072,768]{1,0:T(8,128)(2,1)} %all-gather.12.cloned.1.call-done, f32[768]{0:T(1024)S(1)} %convert_element_type.215, pred[1024]{0:T(1024)(128)(4,1)S(1)} %copy-done.70), kind=kOutput, calls=%fused_computation.94 | convolution fusion | flops 4834983936 | bytes 15732736 | tf_op jit(solution)/shard_map/dot_general | solution.py:198
  759.1 74.7 %all-reduce.25.cloned.1.call-done = (bf16[192,2304]{1,0:T(8,128)(2,1)}, bf16[192,768]{1,0:T(8,128)(2,1)}, bf16[192,3072]{1,0:T(8,128)(2,1)}, bf16[768,768]{1,0:T(8,128)(2,1)}) async-done(((bf16[192,2304]{1,0:T(8,128)(2,1)}, bf16[192,768]{1,0:T(8,128)(2,1)}, bf16[192,3072]{1,0:T(8,128)(2,1)}, bf16[768,768]{1,0:T(8,128)(2,1)}), (bf16[192,2304]{1,0:T(8,128)(2,1)}, bf16[192,768]{1,0:T(8,128)(2,1)}, ...) | async-done | bytes 3538960 | tf_op jit(solution)/shard_map/psum | solution.py:304
  (378 shorter events, 142.5 us)
Async XLA Ops:
  7.3 7.2 copy-start.86
  7.3 26.5 %copy-start.35 = (bf16[1024,768]{1,0:T(8,128)(2,1)S(1)}, bf16[1024,768]{1,0:T(8,128)(2,1)}, u32[]{:S(2)}) copy-start(bf16[1024,768]{1,0:T(8,128)(2,1)} %param.21) | copy-start | bytes 4718596
  7.3 52.9 %all-gather.6.cloned.1.call-start = ((), (), s32[]{:S(2)}) async-start(), calls=%async_computation.4 | async-start | bytes 4423680 | tf_op jit(solution)/shard_map/all_gather | solution.py:131
  8.0 163.9 %all-gather.8.cloned.1.call-start = ((), (), s32[]{:S(2)}) async-start(), calls=%async_computation.5 | async-start | bytes 1474560 | tf_op jit(solution)/shard_map/all_gather | solution.py:133
  8.8 179.9 %all-gather.10.cloned.1.call-start = ((), (), s32[]{:S(2)}) async-start(), calls=%async_computation.6 | async-start | bytes 5898240 | tf_op jit(solution)/shard_map/all_gather | solution.py:135
  9.5 217.4 %all-gather.12.cloned.1.call-start = ((), (), s32[]{:S(2)}) async-start(), calls=%async_computation.7 | async-start | bytes 5898240 | tf_op jit(solution)/shard_map/all_gather | solution.py:137
  10.1 652.6 %reduce-scatter.7.cloned.1.call-start = ((), (), s32[]{:S(2)}) async-start(), calls=%async_computation.9 | async-start | bytes 1474560 | tf_op jit(solution)/shard_map/reduce_scatter | solution.py:266
  33.7 26.4 %copy-start.53 = (f32[768]{0:T(1024)}, f32[768]{0:T(1024)S(1)}, u32[]{:S(2)}) copy-start(f32[768]{0:T(1024)S(1)} %convert_element_type.198) | copy-start | bytes 9220
  33.7 26.4 %copy-start.79 = (f32[768]{0:T(1024)}, f32[768]{0:T(1024)S(1)}, u32[]{:S(2)}) copy-start(f32[768]{0:T(1024)S(1)} %convert_element_type.199) | copy-start | bytes 9220
  33.8 11.9 %copy-start.41 = (s32[1024]{0:T(1024)S(1)}, s32[1024]{0:T(1024)}, u32[]{:S(2)}) copy-start(s32[1024]{0:T(1024)} %param.22) | copy-start | bytes 12292
  34.5 25.6 %copy-start.11 = (bf16[1024,768]{0,1:T(8,128)(2,1)}, bf16[1024,768]{0,1:T(8,128)(2,1)S(1)}, u32[]{:S(2)}) copy-start(bf16[1024,768]{0,1:T(8,128)(2,1)S(1)} %copy.78) | copy-start | bytes 4718596
  34.6 11.6 %copy-start.36 = (bf16[1024,768]{1,0:T(8,128)(2,1)S(1)}, bf16[1024,768]{1,0:T(8,128)(2,1)}, u32[]{:S(2)}) copy-start(bf16[1024,768]{1,0:T(8,128)(2,1)} %param.23) | copy-start | bytes 4718596
  34.8 31.6 %copy-start.51 = (f32[1024]{0:T(1024)}, f32[1024]{0:T(1024)S(1)}, u32[]{:S(2)}) copy-start(f32[1024]{0:T(1024)S(1)} %broadcast_multiply_fusion.3) | copy-start | bytes 12292
  35.3 31.1 %copy-start.57 = (f32[1024]{0:T(1024)}, f32[1024]{0:T(1024)S(1)}, u32[]{:S(2)}) copy-start(f32[1024]{0:T(1024)S(1)} %fusion.54) | copy-start | bytes 12292
  35.4 53.1 %copy-start.77 = (f32[64]{0:T(128)}, f32[64]{0:T(128)S(1)}, u32[]{:S(2)}) copy-start(f32[64]{0:T(128)S(1)} %convert_element_type.202) | copy-start | bytes 772
  35.4 53.1 %copy-start.71 = (f32[64]{0:T(128)}, f32[64]{0:T(128)S(1)}, u32[]{:S(2)}) copy-start(f32[64]{0:T(128)S(1)} %convert_element_type.204) | copy-start | bytes 772
  76.1 12.4 %copy-start.32 = (f32[1024,12]{0,1:T(8,128)}, f32[1024,12]{0,1:T(8,128)S(1)}, u32[]{:S(2)}) copy-start(f32[1024,12]{0,1:T(8,128)S(1)} %broadcast_multiply_fusion.1) | copy-start | bytes 147460
  81.1 7.3 copy-start.43
  94.6 23.8 %copy-start.10 = (bf16[1024,12,64]{0,2,1:T(8,128)(2,1)S(1)}, bf16[1024,12,64]{0,2,1:T(8,128)(2,1)}, u32[]{:S(2)}) copy-start(bf16[1024,12,64]{0,2,1:T(8,128)(2,1)} %get-tuple-element.490) | copy-start | bytes 4718596 | tf_op jit(solution)/shard_map/while
  106.1 15.8 %copy-start = (f32[12,512,1024]{2,1,0:T(8,128)S(1)}, f32[12,512,1024]{2,1,0:T(8,128)}, u32[]{:S(2)}) copy-start(f32[12,512,1024]{2,1,0:T(8,128)} %get-tuple-element.444) | copy-start | bytes 75497472 | tf_op jit(solution)/shard_map/while
  132.1 23.0 %copy-start.10 = (bf16[1024,12,64]{0,2,1:T(8,128)(2,1)S(1)}, bf16[1024,12,64]{0,2,1:T(8,128)(2,1)}, u32[]{:S(2)}) copy-start(bf16[1024,12,64]{0,2,1:T(8,128)(2,1)} %get-tuple-element.490) | copy-start | bytes 4718596 | tf_op jit(solution)/shard_map/while
  142.7 16.1 %copy-start = (f32[12,512,1024]{2,1,0:T(8,128)S(1)}, f32[12,512,1024]{2,1,0:T(8,128)}, u32[]{:S(2)}) copy-start(f32[12,512,1024]{2,1,0:T(8,128)} %get-tuple-element.444) | copy-start | bytes 75497472 | tf_op jit(solution)/shard_map/while
  175.8 88.6 %copy-start.55 = (f32[1024]{0:T(1024)}, f32[1024]{0:T(1024)S(1)}, u32[]{:S(2)}) copy-start(f32[1024]{0:T(1024)S(1)} %broadcast_multiply_fusion.2) | copy-start | bytes 12292
  176.7 87.7 %copy-start.65 = (f32[1024]{0:T(1024)}, f32[1024]{0:T(1024)S(1)}, u32[]{:S(2)}) copy-start(f32[1024]{0:T(1024)S(1)} %fusion.55) | copy-start | bytes 12292
  188.7 38.2 %copy-start.69 = (pred[1024]{0:T(1024)(128)(4,1)S(1)}, pred[1024]{0:T(1024)(128)(4,1)}, u32[]{:S(2)}) copy-start(pred[1024]{0:T(1024)(128)(4,1)} %broadcast_compare_fusion.2) | copy-start | bytes 3076
  270.7 11.5 %copy-start.6 = (bf16[1024,12,64]{0,2,1:T(8,128)(2,1)}, bf16[1024,12,64]{0,2,1:T(8,128)(2,1)S(1)}, u32[]{:S(2)}) copy-start(bf16[1024,12,64]{0,2,1:T(8,128)(2,1)S(1)} %get-tuple-element.530) | copy-start | bytes 4718596 | tf_op jit(solution)/shard_map/while
  282.7 18.3 %copy-start.4 = (pred[512,1024]{1,0:T(8,128)(4,1)}, pred[512,1024]{1,0:T(8,128)(4,1)S(1)}, u32[]{:S(2)}) copy-start(pred[512,1024]{1,0:T(8,128)(4,1)S(1)} %broadcast_compare_fusion.6) | copy-start | bytes 1572868 | tf_op jit(solution)/shard_map/while
  363.7 8.9 %copy-start.5 = (pred[512,1024]{1,0:T(8,128)(4,1)S(1)}, pred[512,1024]{1,0:T(8,128)(4,1)}, u32[]{:S(2)}) copy-start(pred[512,1024]{1,0:T(8,128)(4,1)} %copy-done.4) | copy-start | bytes 1572868 | tf_op jit(solution)/shard_map/while
  363.7 8.9 %copy-start.23 = (bf16[1024,12,64]{0,2,1:T(8,128)(2,1)S(1)}, bf16[1024,12,64]{0,2,1:T(8,128)(2,1)}, u32[]{:S(2)}) copy-start(bf16[1024,12,64]{0,2,1:T(8,128)(2,1)} %get-tuple-element.534) | copy-start | bytes 4718596 | tf_op jit(solution)/shard_map/while
  372.6 13.4 %copy-start.7 = (bf16[1024,12,64]{0,2,1:T(8,128)(2,1)S(1)}, bf16[1024,12,64]{0,2,1:T(8,128)(2,1)}, u32[]{:S(2)}) copy-start(bf16[1024,12,64]{0,2,1:T(8,128)(2,1)} %copy-done.6) | copy-start | bytes 4718596 | tf_op jit(solution)/shard_map/while
  386.0 11.5 %copy-start.6 = (bf16[1024,12,64]{0,2,1:T(8,128)(2,1)}, bf16[1024,12,64]{0,2,1:T(8,128)(2,1)S(1)}, u32[]{:S(2)}) copy-start(bf16[1024,12,64]{0,2,1:T(8,128)(2,1)S(1)} %get-tuple-element.530) | copy-start | bytes 4718596 | tf_op jit(solution)/shard_map/while
  397.9 18.3 %copy-start.4 = (pred[512,1024]{1,0:T(8,128)(4,1)}, pred[512,1024]{1,0:T(8,128)(4,1)S(1)}, u32[]{:S(2)}) copy-start(pred[512,1024]{1,0:T(8,128)(4,1)S(1)} %broadcast_compare_fusion.6) | copy-start | bytes 1572868 | tf_op jit(solution)/shard_map/while
  478.9 9.8 %copy-start.5 = (pred[512,1024]{1,0:T(8,128)(4,1)S(1)}, pred[512,1024]{1,0:T(8,128)(4,1)}, u32[]{:S(2)}) copy-start(pred[512,1024]{1,0:T(8,128)(4,1)} %copy-done.4) | copy-start | bytes 1572868 | tf_op jit(solution)/shard_map/while
  478.9 9.8 %copy-start.23 = (bf16[1024,12,64]{0,2,1:T(8,128)(2,1)S(1)}, bf16[1024,12,64]{0,2,1:T(8,128)(2,1)}, u32[]{:S(2)}) copy-start(bf16[1024,12,64]{0,2,1:T(8,128)(2,1)} %get-tuple-element.534) | copy-start | bytes 4718596 | tf_op jit(solution)/shard_map/while
  488.7 14.3 %copy-start.7 = (bf16[1024,12,64]{0,2,1:T(8,128)(2,1)S(1)}, bf16[1024,12,64]{0,2,1:T(8,128)(2,1)}, u32[]{:S(2)}) copy-start(bf16[1024,12,64]{0,2,1:T(8,128)(2,1)} %copy-done.6) | copy-start | bytes 4718596 | tf_op jit(solution)/shard_map/while
  548.9 113.8 %reduce-scatter.5.cloned.1.call-start = ((), (), s32[]{:S(2)}) async-start(), calls=%async_computation.8 | async-start | bytes 4423680 | tf_op jit(solution)/shard_map/reduce_scatter | solution.py:260
  555.1 12.4 %copy-start.24 = (bf16[1024,768]{1,0:T(8,128)(2,1)}, bf16[1024,768]{1,0:T(8,128)(2,1)S(1)}, u32[]{:S(2)}) copy-start(bf16[1024,768]{1,0:T(8,128)(2,1)S(1)} %copy.95) | copy-start | bytes 4718596
  559.4 9.3 %copy-start.12 = (bf16[1024,768]{0,1:T(8,128)(2,1)S(1)}, bf16[1024,768]{0,1:T(8,128)(2,1)}, u32[]{:S(2)}) copy-start(bf16[1024,768]{0,1:T(8,128)(2,1)} %copy-done.11) | copy-start | bytes 4718596
  559.4 9.3 %copy-start.26 = (bf16[1024,768]{1,0:T(8,128)(2,1)S(1)}, bf16[1024,768]{1,0:T(8,128)(2,1)}, u32[]{:S(2)}) copy-start(bf16[1024,768]{1,0:T(8,128)(2,1)} %copy.96) | copy-start | bytes 4718596
  559.4 9.3 %copy-start.52 = (f32[1024]{0:T(1024)S(1)}, f32[1024]{0:T(1024)}, u32[]{:S(2)}) copy-start(f32[1024]{0:T(1024)} %copy-done.51) | copy-start | bytes 12292
  559.4 9.3 %copy-start.54 = (f32[768]{0:T(1024)S(1)}, f32[768]{0:T(1024)}, u32[]{:S(2)}) copy-start(f32[768]{0:T(1024)} %copy-done.53) | copy-start | bytes 9220
  559.4 9.3 %copy-start.58 = (f32[1024]{0:T(1024)S(1)}, f32[1024]{0:T(1024)}, u32[]{:S(2)}) copy-start(f32[1024]{0:T(1024)} %copy-done.57) | copy-start | bytes 12292
  559.4 9.3 %copy-start.80 = (f32[768]{0:T(1024)S(1)}, f32[768]{0:T(1024)}, u32[]{:S(2)}) copy-start(f32[768]{0:T(1024)} %copy-done.79) | copy-start | bytes 9220
  574.7 112.4 %reduce-scatter.9.cloned.1.call-start = ((), (), s32[]{:S(2)}) async-start(), calls=%async_computation.10 | async-start | bytes 5898240 | tf_op jit(solution)/shard_map/reduce_scatter | solution.py:272
  585.3 161.8 %reduce-scatter.11.cloned.1.call-start = ((), (), s32[]{:S(2)}) async-start(), calls=%async_computation.11 | async-start | bytes 5898240 | tf_op jit(solution)/shard_map/reduce_scatter | solution.py:278
  596.9 237.0 %all-reduce.25.cloned.1.call-start = ((), (), s32[]{:S(2)}) async-start(), calls=%async_computation.12 | async-start | bytes 7077888 | tf_op jit(solution)/shard_map/psum | solution.py:304
  617.9 36.4 %copy-start.60 = (f32[1024]{0:T(1024)S(1)}, f32[1024]{0:T(1024)}, u32[]{:S(2)}) copy-start(f32[1024]{0:T(1024)} %copy-done.59) | copy-start | bytes 12292
  660.0 87.1 %copy-start.16 = (f32[1024,768]{0,1:T(8,128)S(1)}, f32[1024,768]{0,1:T(8,128)}, u32[]{:S(2)}) copy-start(f32[1024,768]{0,1:T(8,128)} %copy-done.14) | copy-start | bytes 9437188
  (65 other events, 218.1 us)
Sparse Core Ops, SparseCore 0:
  9.9 50.1 all-gather.5
  62.0 27.5 all-gather.7
  91.4 56.9 all-gather.9
  150.1 56.9 all-gather.11
  549.1 27.3 reduce-scatter.6
  579.4 47.5 reduce-scatter.4
  630.0 57.0 reduce-scatter.8
  690.0 56.9 reduce-scatter.10
  749.7 84.1 all-reduce.24
where the time goes:
time: 856 us; the launch traced here: 848 us
  matrix products  291 us (34%)
  waiting for transfers between devices  173 us (20%)
  local copies, waits for them, and re-layouts  162 us (19%)
  other arithmetic  141 us (16%)
  blocking collectives  55.5 us (6%)
  between operations  20 us (2%)
    psum x1, waiting for transfers between devices, shards(): lax.psum(summed[0].astype(jnp.bfloat16), 'dp').astype(jnp.float32)  74.7 us
    dynamic_update_slice x4, local copies, waits for them, and re-layouts, attend(): lax.map(one_block, jnp.arange(count // block, dtype=jnp.int32))  63.6 us
    reduce_scatter x1, waiting for transfers between devices, shards(): lax.psum_scatter(down_grad.astype(jnp.bfloat16), 'fsdp', scatter_dimensio...  60 us
    convert_element_type x2, other arithmetic, one_block(): scores_low = grad_scores.astype(jnp.bfloat16)  42.4 us
    dot_general x4, matrix products, block_scores(): jnp.einsum('qhe,khe->hqk', query_block, key_low, preferred_element_type=j...  42.4 us
    dot_general x4, matrix products, right_product(): lax.dot_general(left, right, (((1,), (1,)), ((), ())), preferred_element_...  41.1 us
    dot_general x1, matrix products, shards(): jnp.dot(second_low, up_matrix, preferred_element_type=jnp.float32)  38.1 us
    dot_general x2, matrix products, one_block(): jnp.einsum('qhe,khe->hqk', grad_block, value_low, preferred_element_type=...  36.5 us
  transfers between devices with their start and end apart: 9, of which 4 were waited for; matrix products, arithmetic and copies ran while one was open for 30% of the time, Pallas kernels for 0%

commit v1 on v0

--- a/solution.py
+++ b/solution.py
@@ -4,6 +4,12 @@
 from jax.sharding import PartitionSpec as P
 
 norm_eps = 1e-06
+
+
+def gather_and_add(value, axis):
+    parts = lax.all_gather(value, axis, axis=0, tiled=False)
+    summed = parts.sum(axis=0)
+    return summed
 
 
 def layer_norm(value, gain, shift):
@@ -301,7 +307,7 @@
         ).astype(jnp.float32),
     )
     final = (
-        lax.psum(summed[0].astype(jnp.bfloat16), "dp").astype(jnp.float32),
+        gather_and_add(summed[0].astype(jnp.bfloat16), "dp").astype(jnp.float32),
         lax.psum(summed[1].astype(jnp.bfloat16), "dp").astype(jnp.float32),
         lax.psum(summed[2].astype(jnp.bfloat16), "dp").astype(jnp.float32),
         lax.psum(summed[3].astype(jnp.bfloat16), "dp").astype(jnp.float32),

time: 856 us -> 806 us (0.942)
  waiting for transfers between devices: 173 us -> 123 us
    psum x1, waiting for transfers between devices: 74.7 us -> 0.01 us  [shards(): lax.psum(summed[2].astype(jnp.bfloat16), 'dp').astype(jnp.float32)]
    all_gather x0 -> x1, waiting for transfers between devices: none -> 61.2 us  [gather_and_add(): parts = lax.all_gather(value, axis, axis=0, tiled=False)]
    reduce_scatter x1, waiting for transfers between devices: 60 us -> 0.02 us  [shards(): lax.psum_scatter(down_grad.astype(jnp.bfloat16), 'fsdp', scatter_dimensio...]
    reduce_scatter x1, waiting for transfers between devices: 0.01 us -> 46.2 us  [shards(): lax.psum_scatter(qkv_grad.astype(jnp.bfloat16), 'fsdp', scatter_dimension...]
    reduce_scatter x1, waiting for transfers between devices: 24.3 us -> 0.02 us  [shards(): lax.psum_scatter(up_grad.astype(jnp.bfloat16), 'fsdp', scatter_dimension=...]
    unnamed x218 -> x220, local copies, waits for them, and re-layouts: 25.4 us -> 26.1 us
  transfers between devices with their start and end apart: 9 -> 10, of which waited for: 4 -> 3; matrix products, arithmetic and copies ran while one was open for 30% -> 66% of each run, Pallas kernels for 0% -> 0%
where the time goes in v1:
time: 806 us; the launch traced here: 797 us
  matrix products  293 us (36%)
  local copies, waits for them, and re-layouts  157 us (19%)
  other arithmetic  144 us (18%)
  waiting for transfers between devices  123 us (15%)
  blocking collectives  56.7 us (7%)
  between operations  20.2 us (3%)
    dynamic_update_slice x4, local copies, waits for them, and re-layouts, attend(): lax.map(one_block, jnp.arange(count // block, dtype=jnp.int32))  63.8 us
    all_gather x1, waiting for transfers between devices, gather_and_add(): parts = lax.all_gather(value, axis, axis=0, tiled=False)  61.2 us
    reduce_scatter x1, waiting for transfers between devices, shards(): lax.psum_scatter(qkv_grad.astype(jnp.bfloat16), 'fsdp', scatter_dimension...  46.2 us
    dot_general x4, matrix products, block_scores(): jnp.einsum('qhe,khe->hqk', query_block, key_low, preferred_element_type=j...  45.4 us
    convert_element_type x2, other arithmetic, one_block(): scores_low = grad_scores.astype(jnp.bfloat16)  44 us
    dot_general x4, matrix products, right_product(): lax.dot_general(left, right, (((1,), (1,)), ((), ())), preferred_element_...  42 us
    dot_general x1, matrix products, shards(): jnp.dot(second_low, up_matrix, preferred_element_type=jnp.float32)  38 us
    dot_general x2, matrix products, one_block(): jnp.einsum('qhe,khe->hqk', grad_block, value_low, preferred_element_type=...  36.9 us
  transfers between devices with their start and end apart: 10, of which 3 were waited for; matrix products, arithmetic and copies ran while one was open for 66% of the time, Pallas kernels for 0%

profile of v1, /device:TPU:0, one launch (start us, length us, event | category | flops | bytes accessed | tf_op | source)
XLA Modules:
  0.0 797.4 jit_solution(11015331963685651000)
XLA Ops:
  14.7 19.0 %all-reduce.22 = (bf16[2304]{0:T(1024)(128)(2,1)S(1)}, bf16[768]{0:T(1024)(128)(2,1)S(1)}, bf16[768]{0:T(1024)(128)(2,1)S(1)}, bf16[64]{0:T(256)(128)(2,1)S(1)},...) all-reduce(bf16[2304]{0:T(1024)(128)(2,1)S(1)} %dynamic-update-slic, ...), channel_id=1, replica_groups=mesh['dp'=8,'fsdp'=4] {'fsdp'}, use_global_device_ids=true, to_apply=%add.2 | all-reduce | flops 6272 | bytes 25088
  37.2 7.8 all-gather.1
  47.9 12.3 %all-gather.8.cloned.1.call-done = bf16[768,2304]{1,0:T(8,128)(2,1)} async-done(((bf16[192,2304]{1,0:T(8,128)(2,1)}), bf16[768,2304]{1,0:T(8,128)(2,1)}) %all-gather.8.cloned.1.call-update) | async-done | bytes 3538960 | tf_op jit(solution)/shard_map/all_gather | solution.py:137
  60.1 6.3 convolution_add_fusion
  84.7 4.1 multiply_convert_fusion.2
  88.9 73.6 %while.27 = (s32[]{:T(128)}, bf16[2,512,12,64]{1,3,2,0:T(8,128)(2,1)}, f32[2,12,512]{2,1,0:T(8,128)S(1)}, s32[2]{0:T(128)S(1)}, s32[1024]{0:T(1024)S(1)}, /*inde...) while((s32[]{:T(128)}, ...), condition=%wide.region_9.10_spmd, body=%wide.region_6.9_spmd.sunk | while | flops 1686628352 | bytes 190286576 | solution.py:73
  90.8 11.5 %fusion.114 = (f32[12,512]{1,0:T(8,128)S(1)}, f32[12,512,1024]{2,1,0:T(8,128)}) fusion(pred[512,1024]{1,0:T(8,128)(4,1)S(1)} %broadcast_compare_fusion.5, bf16[1024,12,64]{0,2,1:T(8,128)(2,1)S(1)} %get-tuple-element.488, bf16[1024,12,64]{0,2,1:T(8,128)(2,1)S(1)} %get-tuple-element.487, s32[]{:T(128)S(6)} %select_n.77), kind=kOutput, calls=%fused_computation.3.clone.1 | convolution fusion | flops 824174592 | bytes 28073988 | tf_op jit(solution)/shard_map/while/body/eval_jaxpr/qhe,khe->hqk/dot_general | solution.py:50
  102.3 12.3 %fusion.115 = f32[12,512]{1,0:T(8,128)S(1)} fusion(f32[12,512,1024]{2,1,0:T(8,128)} %get-tuple-element.443, f32[12,512]{1,0:T(8,128)S(1)} %get-tuple-element.444, pred[512,1024]{1,0:T(8,128)(4,1)S(1)} %broadcast_compare_fusion.5), kind=kLoop, calls=%fused_computation.4.clone.1 | loop fusion | flops 25159680 | bytes 25739264 | tf_op jit(solution)/shard_map/while/body/eval_jaxpr/reduce_sum | solution.py:66
  117.7 8.5 %bitcast_dynamic-update-slice_fusion.4 = bf16[2,512,12,64]{1,3,2,0:T(8,128)(2,1)} fusion(bf16[2,512,12,64]{1,3,2,0:T(8,128)(2,1)} %get-tuple-element.471, s32[]{:T(128)} %get-tuple-element.470, bf16[1024,12,64]{0,2,1:T(8,128)(2,1)S(1)} %copy-done.12, f32[12,512,1024]{2,1,0:T(8,128)S(1)} %copy-done, f32[12,512]{1,0:T(8,128)S(1)} %fusion.115, ...), kind=kOutput, calls=%fused_computation.6.clone.1 | convolution fusion | flops 836763648 | bytes 28885504 | tf_op jit(solution)/shard_map/while/body/eval_jaxpr/hqk,khe->qhe/dot_general | solution.py:68
  127.9 10.7 %fusion.114 = (f32[12,512]{1,0:T(8,128)S(1)}, f32[12,512,1024]{2,1,0:T(8,128)}) fusion(pred[512,1024]{1,0:T(8,128)(4,1)S(1)} %broadcast_compare_fusion.5, bf16[1024,12,64]{0,2,1:T(8,128)(2,1)S(1)} %get-tuple-element.488, bf16[1024,12,64]{0,2,1:T(8,128)(2,1)S(1)} %get-tuple-element.487, s32[]{:T(128)S(6)} %select_n.77), kind=kOutput, calls=%fused_computation.3.clone.1 | convolution fusion | flops 824174592 | bytes 28073988 | tf_op jit(solution)/shard_map/while/body/eval_jaxpr/qhe,khe->hqk/dot_general | solution.py:50
  138.6 12.3 %fusion.115 = f32[12,512]{1,0:T(8,128)S(1)} fusion(f32[12,512,1024]{2,1,0:T(8,128)} %get-tuple-element.443, f32[12,512]{1,0:T(8,128)S(1)} %get-tuple-element.444, pred[512,1024]{1,0:T(8,128)(4,1)S(1)} %broadcast_compare_fusion.5), kind=kLoop, calls=%fused_computation.4.clone.1 | loop fusion | flops 25159680 | bytes 25739264 | tf_op jit(solution)/shard_map/while/body/eval_jaxpr/reduce_sum | solution.py:66
  154.0 8.5 %bitcast_dynamic-update-slice_fusion.4 = bf16[2,512,12,64]{1,3,2,0:T(8,128)(2,1)} fusion(bf16[2,512,12,64]{1,3,2,0:T(8,128)(2,1)} %get-tuple-element.471, s32[]{:T(128)} %get-tuple-element.470, bf16[1024,12,64]{0,2,1:T(8,128)(2,1)S(1)} %copy-done.12, f32[12,512,1024]{2,1,0:T(8,128)S(1)} %copy-done, f32[12,512]{1,0:T(8,128)S(1)} %fusion.115, ...), kind=kOutput, calls=%fused_computation.6.clone.1 | convolution fusion | flops 836763648 | bytes 28885504 | tf_op jit(solution)/shard_map/while/body/eval_jaxpr/hqk,khe->qhe/dot_general | solution.py:68
  162.5 4.2 copy.82
  168.3 3.8 fusion.71
  172.9 38.0 %multiply_convert_fusion.1 = (bf16[1024,3072]{1,0:T(8,128)(2,1)}, f32[1024,3072]{1,0:T(8,128)}, f32[1024,3072]{1,0:T(8,128)}) fusion(f32[3072]{0:T(1024)S(1)} %bitcast.139, bf16[768,3072]{1,0:T(8,128)(2,1)} %all-gather.12.cloned.1.call-done, f32[1024,768]{0,1:T(8,128)S(1)} %get-tuple-element.324, f32[768]{0:T(1024)S(1)} %copy-done.80, ...), kind=kOutput, calls=%fused_computation.40 | convolution fusion | flops 5043388416 | bytes 39348224 | tf_op jit(solution)/shard_map/dot_general | solution.py:199
  210.9 19.4 %fusion.72 = (bf16[3072]{0:T(1024)(128)(2,1)}, bf16[1024,3072]{1,0:T(8,128)(2,1)}) fusion(f32[1024,3072]{1,0:T(8,128)} %get-tuple-element.309, bf16[3072,768]{1,0:T(8,128)(2,1)} %all-gather.14.cloned.1.call-done, bf16[1024,768]{0,1:T(8,128)(2,1)} %copy.84, pred[1024]{0:T(1024)(128)(4,1)S(1)} %copy-done.68, f32[1024,3072]{1,0:T(8,128)} %get-tuple-element.325, ...), kind=kOutput, calls=%fused_computation.139 | convolution fusion | flops 4884526080 | bytes 37768192 | tf_op jit(solution)/shard_map/dot_general | solution.py:43
  230.3 10.3 %fusion.74 = (bf16[768]{0:T(1024)(128)(2,1)}, f32[1024,768]{1,0:T(8,128)}) fusion(bf16[1024,3072]{1,0:T(8,128)(2,1)} %get-tuple-element.327, bf16[768,3072]{1,0:T(8,128)(2,1)} %all-gather.12.cloned.1.call-done), kind=kOutput, calls=%fused_computation.141 | convolution fusion | flops 4832623616 | bytes 14157312 | tf_op jit(solution)/shard_map/dot_general | solution.py:43
  254.1 9.8 %convolution_convert_fusion.1 = bf16[768,3072]{1,0:T(8,128)(2,1)} fusion(bf16[1024,3072]{1,0:T(8,128)(2,1)} %get-tuple-element.327, f32[1024,768]{0,1:T(8,128)S(1)} %get-tuple-element.324, f32[768]{0:T(1024)S(1)} %copy-done.80, f32[768]{0:T(1024)S(1)} %copy-done.65, f32[1024]{0:T(1024)S(1)} %fusion.55, f32[1024]{0:T(1024)S(1)} %broadcast_multiply_fusion.2), kind=kOutput, calls=%fused_computation.56 | convolution fusion | flops 4838129664 | bytes 14170112 | tf_op jit(solution)/shard_map/dot_general | solution.py:37
  265.9 3.7 reshape.305
  278.1 9.8 %convolution_convert_fusion = bf16[3072,768]{1,0:T(8,128)(2,1)} fusion(bf16[1024,3072]{1,0:T(8,128)(2,1)} %get-tuple-element.308, bf16[1024,768]{0,1:T(8,128)(2,1)S(1)} %copy-done.22, pred[1024]{0:T(1024)(128)(4,1)S(1)} %copy-done.68), kind=kOutput, calls=%fused_computation.55 | convolution fusion | flops 4836556800 | bytes 12583936 | tf_op jit(solution)/shard_map/dot_general | solution.py:37
  289.3 3.8 convolution_convert_fusion.3
  293.1 238.3 %while.28 = (s32[]{:T(128)}, f32[1024,12,64]{0,2,1:T(8,128)}, f32[1024,12,64]{0,2,1:T(8,128)}, f32[2,512,12,64]{1,0,3,2:T(2,128)}, s32[2]{0:T(128)S(1)}, /*index...) while((s32[]{:T(128)}, f32[1024,12,64]{0,2,1:T(8,128)}, ...), condition=%wide.region_16.17_spmd.clone, body=%wide.region_14.16_spmd.clone.sunk | while | flops 4125747200 | bytes 229828944 | solution.py:111
  294.8 11.8 %fusion.125 = f32[12,512,1024]{2,1,0:T(8,128)} fusion(bf16[1024,12,64]{0,2,1:T(8,128)(2,1)S(1)} %get-tuple-element.531, bf16[1024,12,64]{0,2,1:T(8,128)(2,1)} %get-tuple-element.529, s32[]{:T(128)S(6)} %select_n.81), kind=kOutput, calls=%fused_computation.28.clone.1 | convolution fusion | flops 805306368 | bytes 27525124 | tf_op jit(solution)/shard_map/while/body/eval_jaxpr/qhe,khe->hqk/dot_general | solution.py:50
  307.1 18.7 %multiply_reduce_fusion.11 = (f32[12,512]{1,0:T(8,128)S(1)}, f32[12,512,1024]{2,1,0:T(8,128)}) fusion(f32[12,512,1024]{2,1,0:T(8,128)} %fusion.125, f32[12,512]{1,0:T(8,128)S(1)} %dynamic-slice_bitcast_fusion.2, pred[512,1024]{1,0:T(8,128)(4,1)S(1)} %broadcast_compare_fusion.6, bf16[1024,12,64]{0,2,1:T(8,128)(2,1)} %get-tuple-element.534, ...), kind=kOutput, calls=%fused_computation.15.clone.1 | convolution fusion | flops 836757504 | bytes 53264388 | tf_op jit(solution)/shard_map/while/body/eval_jaxpr/qhe,khe->hqk/dot_general | solution.py:95
  325.8 22.7 %multiply_convert_fusion.5 = bf16[12,512,1024]{2,1,0:T(8,128)(2,1)} fusion(f32[12,512,1024]{2,1,0:T(8,128)} %get-tuple-element.456, f32[12,512,1024]{2,1,0:T(8,128)} %fusion.125, f32[12,512]{1,0:T(8,128)S(1)} %get-tuple-element.457, f32[12,512]{1,0:T(8,128)S(1)} %dynamic-slice_bitcast_fusion.2, pred[512,1024]{1,0:T(8,128)(4,1)S(1)} %broadcast_compare_fusion.6), kind=kLoop, calls=%fused_computation.14.clone.1 | loop fusion | flops 37748736 | bytes 63488000 | tf_op jit(solution)/shard_map/while/body/eval_jaxpr/convert_element_type | solution.py:101
  348.5 10.3 %multiply_bitcast_fusion.3 = f32[1,512,12,64]{1,3,2,0:T(8,128)} fusion(bf16[12,512,1024]{2,1,0:T(8,128)(2,1)} %multiply_convert_fusion.5, bf16[1024,12,64]{0,2,1:T(8,128)(2,1)S(1)} %get-tuple-element.531), kind=kOutput, calls=%fused_computation.22.clone.1 | convolution fusion | flops 805699584 | bytes 15728640 | tf_op jit(solution)/shard_map/while/body/eval_jaxpr/hqk,khe->qhe/dot_general | solution.py:102
  362.1 28.8 %dynamic_update_slice.19 = f32[2,512,12,64]{1,0,3,2:T(2,128)} dynamic-update-slice(f32[2,512,12,64]{1,0,3,2:T(2,128)} %get-tuple-element.512, f32[1,512,12,64]{1,0,3,2:T(1,128)S(1)} %copy.132, s32[]{:T(128)} %get-tuple-element.509, s32[]{:T(128)} %constant.71.clone.1..sunk.1, s32[]{:T(128)} %constant.71.clone.1..sunk.1, s32[]{:T(128)} %constant.71.clone.1..sunk.1) | dynamic-update-slice | bytes 3145732 | tf_op jit(solution)/shard_map/while/body/jit(dynamic_update_index_in_dim)/dynamic_update_slice | solution.py:73
  390.9 9.0 %bitcast_add_fusion.4 = f32[1024,12,64]{0,2,1:T(8,128)} fusion(f32[1024,12,64]{0,2,1:T(8,128)} %get-tuple-element.510, bf16[12,512,1024]{2,1,0:T(8,128)(2,1)} %multiply_convert_fusion.5, pred[]{:T(512)S(6)} %compare.3, bf16[1024,12,64]{0,2,1:T(8,128)(2,1)} %get-tuple-element.529, s32[]{:T(128)S(6)} %select_n.81), kind=kOutput, calls=%fused_computation.21.clone.1 | convolution fusion | flops 807665664 | bytes 19660804 | tf_op jit(solution)/shard_map/while/body/eval_jaxpr/hqk,qhe->khe/dot_general | solution.py:105
  399.9 13.4 %bitcast_add_fusion.5 = f32[1024,12,64]{0,2,1:T(8,128)} fusion(f32[1024,12,64]{0,2,1:T(8,128)} %get-tuple-element.511, f32[12,512,1024]{2,1,0:T(8,128)} %fusion.125, f32[12,512]{1,0:T(8,128)S(1)} %dynamic-slice_bitcast_fusion.2, pred[512,1024]{1,0:T(8,128)(4,1)S(1)} %copy-done.7, pred[]{:T(512)S(6)} %compare.3, ...), kind=kOutput, calls=%fused_computation.20.clone.1 | convolution fusion | flops 832045056 | bytes 32800772 | tf_op jit(solution)/shard_map/while/body/eval_jaxpr/hqk,qhe->khe/dot_general | solution.py:89
  414.6 11.4 %fusion.125 = f32[12,512,1024]{2,1,0:T(8,128)} fusion(bf16[1024,12,64]{0,2,1:T(8,128)(2,1)S(1)} %get-tuple-element.531, bf16[1024,12,64]{0,2,1:T(8,128)(2,1)} %get-tuple-element.529, s32[]{:T(128)S(6)} %select_n.81), kind=kOutput, calls=%fused_computation.28.clone.1 | convolution fusion | flops 805306368 | bytes 27525124 | tf_op jit(solution)/shard_map/while/body/eval_jaxpr/qhe,khe->hqk/dot_general | solution.py:50
  426.4 18.3 %multiply_reduce_fusion.11 = (f32[12,512]{1,0:T(8,128)S(1)}, f32[12,512,1024]{2,1,0:T(8,128)}) fusion(f32[12,512,1024]{2,1,0:T(8,128)} %fusion.125, f32[12,512]{1,0:T(8,128)S(1)} %dynamic-slice_bitcast_fusion.2, pred[512,1024]{1,0:T(8,128)(4,1)S(1)} %broadcast_compare_fusion.6, bf16[1024,12,64]{0,2,1:T(8,128)(2,1)} %get-tuple-element.534, ...), kind=kOutput, calls=%fused_computation.15.clone.1 | convolution fusion | flops 836757504 | bytes 53264388 | tf_op jit(solution)/shard_map/while/body/eval_jaxpr/qhe,khe->hqk/dot_general | solution.py:95
  444.7 21.2 %multiply_convert_fusion.5 = bf16[12,512,1024]{2,1,0:T(8,128)(2,1)} fusion(f32[12,512,1024]{2,1,0:T(8,128)} %get-tuple-element.456, f32[12,512,1024]{2,1,0:T(8,128)} %fusion.125, f32[12,512]{1,0:T(8,128)S(1)} %get-tuple-element.457, f32[12,512]{1,0:T(8,128)S(1)} %dynamic-slice_bitcast_fusion.2, pred[512,1024]{1,0:T(8,128)(4,1)S(1)} %broadcast_compare_fusion.6), kind=kLoop, calls=%fused_computation.14.clone.1 | loop fusion | flops 37748736 | bytes 63488000 | tf_op jit(solution)/shard_map/while/body/eval_jaxpr/convert_element_type | solution.py:101
  465.9 9.6 %multiply_bitcast_fusion.3 = f32[1,512,12,64]{1,3,2,0:T(8,128)} fusion(bf16[12,512,1024]{2,1,0:T(8,128)(2,1)} %multiply_convert_fusion.5, bf16[1024,12,64]{0,2,1:T(8,128)(2,1)S(1)} %get-tuple-element.531), kind=kOutput, calls=%fused_computation.22.clone.1 | convolution fusion | flops 805699584 | bytes 15728640 | tf_op jit(solution)/shard_map/while/body/eval_jaxpr/hqk,khe->qhe/dot_general | solution.py:102
  478.6 28.7 %dynamic_update_slice.19 = f32[2,512,12,64]{1,0,3,2:T(2,128)} dynamic-update-slice(f32[2,512,12,64]{1,0,3,2:T(2,128)} %get-tuple-element.512, f32[1,512,12,64]{1,0,3,2:T(1,128)S(1)} %copy.132, s32[]{:T(128)} %get-tuple-element.509, s32[]{:T(128)} %constant.71.clone.1..sunk.1, s32[]{:T(128)} %constant.71.clone.1..sunk.1, s32[]{:T(128)} %constant.71.clone.1..sunk.1) | dynamic-update-slice | bytes 3145732 | tf_op jit(solution)/shard_map/while/body/jit(dynamic_update_index_in_dim)/dynamic_update_slice | solution.py:73
  507.3 9.8 %bitcast_add_fusion.4 = f32[1024,12,64]{0,2,1:T(8,128)} fusion(f32[1024,12,64]{0,2,1:T(8,128)} %get-tuple-element.510, bf16[12,512,1024]{2,1,0:T(8,128)(2,1)} %multiply_convert_fusion.5, pred[]{:T(512)S(6)} %compare.3, bf16[1024,12,64]{0,2,1:T(8,128)(2,1)} %get-tuple-element.529, s32[]{:T(128)S(6)} %select_n.81), kind=kOutput, calls=%fused_computation.21.clone.1 | convolution fusion | flops 807665664 | bytes 19660804 | tf_op jit(solution)/shard_map/while/body/eval_jaxpr/hqk,qhe->khe/dot_general | solution.py:105
  517.1 14.2 %bitcast_add_fusion.5 = f32[1024,12,64]{0,2,1:T(8,128)} fusion(f32[1024,12,64]{0,2,1:T(8,128)} %get-tuple-element.511, f32[12,512,1024]{2,1,0:T(8,128)} %fusion.125, f32[12,512]{1,0:T(8,128)S(1)} %dynamic-slice_bitcast_fusion.2, pred[512,1024]{1,0:T(8,128)(4,1)S(1)} %copy-done.7, pred[]{:T(512)S(6)} %compare.3, ...), kind=kOutput, calls=%fused_computation.20.clone.1 | convolution fusion | flops 832045056 | bytes 32800772 | tf_op jit(solution)/shard_map/while/body/eval_jaxpr/hqk,qhe->khe/dot_general | solution.py:89
  531.5 5.8 reshape.304
  540.3 10.4 %multiply_reduce_fusion.2 = (bf16[64]{0:T(256)(128)(2,1)S(1)}, f32[2,512,12]{1,0,2:T(2,128)S(1)}) fusion(f32[2,512,12,64]{1,0,3,2:T(2,128)} %get-tuple-element.120, f32[2,512,12,64]{1,0,3,2:T(2,128)} %reshape.305, f32[2,512,12]{1,0,2:T(2,128)S(1)} %copy-done.54, f32[2,512,12]{1,0,2:T(2,128)S(1)} %get-tuple-element.320, ...), kind=kLoop, calls=%fused_computation.84 | loop fusion | flops 7851968 | bytes 6488448 | tf_op jit(solution)/shard_map/transpose(jvp())/reduce_sum | solution.py:24
  578.2 7.8 fusion.45
  587.3 5.8 convolution_convert_fusion.2
  593.9 46.2 %reduce-scatter.5.cloned.1.call-done = bf16[192,2304]{1,0:T(8,128)(2,1)} async-done(((bf16[768,2304]{1,0:T(8,128)(2,1)}), bf16[192,2304]{1,0:T(8,128)(2,1)}) %reduce-scatter.5.cloned.1.call-update) | async-done | bytes 884752 | tf_op jit(solution)/shard_map/reduce_scatter | solution.py:266
  642.9 8.5 %fusion.73 = (bf16[768]{0:T(1024)(128)(2,1)S(1)}, f32[1024,768]{1,0:T(8,128)}) fusion(bf16[768,2304]{1,0:T(8,128)(2,1)} %all-gather.8.cloned.1.call-done, bf16[1024,768]{1,0:T(8,128)(2,1)} %copy.96, bf16[1024,768]{1,0:T(8,128)(2,1)S(1)} %copy.95, bf16[1024,768]{1,0:T(8,128)(2,1)} %copy-done.28), kind=kOutput, calls=%fused_computation.140 | convolution fusion | flops 3638820096 | bytes 11404800 | tf_op jit(solution)/shard_map/dot_general | solution.py:43
  661.1 15.5 %all-reduce.21 = (bf16[768]{0:T(1024)(128)(2,1)S(1)}, bf16[2304]{0:T(1024)(128)(2,1)S(1)}, bf16[768]{0:T(1024)(128)(2,1)S(1)}, bf16[3072]{0:T(1024)(128)(2,1)S(1...) all-reduce(bf16[768]{0:T(1024)(128)(2,1)S(1)} %dynamic-update-slice, ...), channel_id=1, replica_groups=mesh['dp'=8,'fsdp'=4] {'fsdp'}, use_global_device_ids=true, to_apply=%add.8 | all-reduce | flops 10880 | bytes 43520
  677.4 14.4 %all-reduce.19 = (bf16[576]{0:T(1024)(128)(2,1)S(1)}, bf16[192]{0:T(256)(128)(2,1)S(1)}, bf16[768]{0:T(1024)(128)(2,1)S(1)}, bf16[192]{0:T(256)(128)(2,1)S(1)}, ...) all-reduce(bf16[576]{0:T(1024)(128)(2,1)S(1)} %dynamic-slice.10, ...), channel_id=1, replica_groups=mesh['dp'=8,'fsdp'=4] {'dp'}, use_global_device_ids=true, to_apply=%region_27.28 | all-reduce | flops 2528 | bytes 10112 | tf_op jit(solution)/shard_map/psum | solution.py:311
  697.3 5.6 add_convert_fusion.1
  705.7 9.6 %select_convert_fusion = bf16[1024,768]{0,1:T(8,128)(2,1)} fusion(f32[1024,768]{0,1:T(8,128)S(1)} %copy-done.17, bf16[1024,3072]{1,0:T(8,128)(2,1)} %get-tuple-element.308, bf16[3072,768]{1,0:T(8,128)(2,1)} %all-gather.14.cloned.1.call-done, f32[768]{0:T(1024)S(1)} %convert_element_type.217, pred[1024]{0:T(1024)(128)(4,1)S(1)} %copy-done.69), kind=kOutput, calls=%fused_computation.94 | convolution fusion | flops 4834983936 | bytes 15732736 | tf_op jit(solution)/shard_map/dot_general | solution.py:204
  723.3 61.2 %all-gather.16.cloned.1.call-done = bf16[1536,2304]{1,0:T(8,128)(2,1)} async-done(((bf16[192,2304]{1,0:T(8,128)(2,1)}), bf16[1536,2304]{1,0:T(8,128)(2,1)}) %all-gather.16.cloned.1.call-update) | async-done | bytes 7077904 | tf_op jit(solution)/shard_map/all_gather | solution.py:10
  784.6 4.4 reduce_sum.351
  (376 shorter events, 134.4 us)
Async XLA Ops:
  7.2 6.7 copy-start.93
  7.3 6.9 copy-start.94
  7.3 7.2 copy-start.84
  7.3 26.5 %copy-start.35 = (bf16[1024,768]{1,0:T(8,128)(2,1)S(1)}, bf16[1024,768]{1,0:T(8,128)(2,1)}, u32[]{:S(2)}) copy-start(bf16[1024,768]{1,0:T(8,128)(2,1)} %param.21) | copy-start | bytes 4718596
  7.3 52.9 %all-gather.8.cloned.1.call-start = ((), (), s32[]{:S(2)}) async-start(), calls=%async_computation.4 | async-start | bytes 4423680 | tf_op jit(solution)/shard_map/all_gather | solution.py:137
  8.0 160.2 %all-gather.10.cloned.1.call-start = ((), (), s32[]{:S(2)}) async-start(), calls=%async_computation.5 | async-start | bytes 1474560 | tf_op jit(solution)/shard_map/all_gather | solution.py:139
  8.8 163.8 %all-gather.12.cloned.1.call-start = ((), (), s32[]{:S(2)}) async-start(), calls=%async_computation.6 | async-start | bytes 5898240 | tf_op jit(solution)/shard_map/all_gather | solution.py:141
  9.5 201.4 %all-gather.14.cloned.1.call-start = ((), (), s32[]{:S(2)}) async-start(), calls=%async_computation.7 | async-start | bytes 5898240 | tf_op jit(solution)/shard_map/all_gather | solution.py:143
  10.1 583.1 %reduce-scatter.7.cloned.1.call-start = ((), (), s32[]{:S(2)}) async-start(), calls=%async_computation.9 | async-start | bytes 1474560 | tf_op jit(solution)/shard_map/reduce_scatter | solution.py:272
  33.7 26.4 %copy-start.57 = (f32[768]{0:T(1024)}, f32[768]{0:T(1024)S(1)}, u32[]{:S(2)}) copy-start(f32[768]{0:T(1024)S(1)} %convert_element_type.200) | copy-start | bytes 9220
  33.7 26.4 %copy-start.78 = (f32[768]{0:T(1024)}, f32[768]{0:T(1024)S(1)}, u32[]{:S(2)}) copy-start(f32[768]{0:T(1024)S(1)} %convert_element_type.201) | copy-start | bytes 9220
  33.8 11.8 %copy-start.43 = (s32[1024]{0:T(1024)S(1)}, s32[1024]{0:T(1024)}, u32[]{:S(2)}) copy-start(s32[1024]{0:T(1024)} %param.22) | copy-start | bytes 12292
  34.6 25.6 %copy-start.13 = (bf16[1024,768]{0,1:T(8,128)(2,1)}, bf16[1024,768]{0,1:T(8,128)(2,1)S(1)}, u32[]{:S(2)}) copy-start(bf16[1024,768]{0,1:T(8,128)(2,1)S(1)} %copy.78) | copy-start | bytes 4718596
  34.6 11.6 %copy-start.36 = (bf16[1024,768]{1,0:T(8,128)(2,1)S(1)}, bf16[1024,768]{1,0:T(8,128)(2,1)}, u32[]{:S(2)}) copy-start(bf16[1024,768]{1,0:T(8,128)(2,1)} %param.23) | copy-start | bytes 4718596
  34.9 31.6 %copy-start.55 = (f32[1024]{0:T(1024)}, f32[1024]{0:T(1024)S(1)}, u32[]{:S(2)}) copy-start(f32[1024]{0:T(1024)S(1)} %broadcast_multiply_fusion.3) | copy-start | bytes 12292
  35.3 31.1 %copy-start.59 = (f32[1024]{0:T(1024)}, f32[1024]{0:T(1024)S(1)}, u32[]{:S(2)}) copy-start(f32[1024]{0:T(1024)S(1)} %fusion.54) | copy-start | bytes 12292
  35.4 49.3 %copy-start.76 = (f32[64]{0:T(128)}, f32[64]{0:T(128)S(1)}, u32[]{:S(2)}) copy-start(f32[64]{0:T(128)S(1)} %convert_element_type.204) | copy-start | bytes 772
  35.4 49.3 %copy-start.70 = (f32[64]{0:T(128)}, f32[64]{0:T(128)S(1)}, u32[]{:S(2)}) copy-start(f32[64]{0:T(128)S(1)} %convert_element_type.206) | copy-start | bytes 772
  76.1 8.6 %copy-start.32 = (f32[1024,12]{0,1:T(8,128)}, f32[1024,12]{0,1:T(8,128)S(1)}, u32[]{:S(2)}) copy-start(f32[1024,12]{0,1:T(8,128)S(1)} %broadcast_multiply_fusion.1) | copy-start | bytes 147460
  77.4 7.3 copy-start.45
  82.1 6.8 copy-start.41
  90.8 23.8 %copy-start.12 = (bf16[1024,12,64]{0,2,1:T(8,128)(2,1)S(1)}, bf16[1024,12,64]{0,2,1:T(8,128)(2,1)}, u32[]{:S(2)}) copy-start(bf16[1024,12,64]{0,2,1:T(8,128)(2,1)} %get-tuple-element.489) | copy-start | bytes 4718596 | tf_op jit(solution)/shard_map/while
  102.3 15.4 %copy-start = (f32[12,512,1024]{2,1,0:T(8,128)S(1)}, f32[12,512,1024]{2,1,0:T(8,128)}, u32[]{:S(2)}) copy-start(f32[12,512,1024]{2,1,0:T(8,128)} %get-tuple-element.443) | copy-start | bytes 75497472 | tf_op jit(solution)/shard_map/while
  127.9 23.0 %copy-start.12 = (bf16[1024,12,64]{0,2,1:T(8,128)(2,1)S(1)}, bf16[1024,12,64]{0,2,1:T(8,128)(2,1)}, u32[]{:S(2)}) copy-start(bf16[1024,12,64]{0,2,1:T(8,128)(2,1)} %get-tuple-element.489) | copy-start | bytes 4718596 | tf_op jit(solution)/shard_map/while
  138.6 15.4 %copy-start = (f32[12,512,1024]{2,1,0:T(8,128)S(1)}, f32[12,512,1024]{2,1,0:T(8,128)}, u32[]{:S(2)}) copy-start(f32[12,512,1024]{2,1,0:T(8,128)} %get-tuple-element.443) | copy-start | bytes 75497472 | tf_op jit(solution)/shard_map/while
  172.1 82.0 %copy-start.16 = (f32[1024,768]{0,1:T(8,128)}, f32[1024,768]{0,1:T(8,128)S(1)}, u32[]{:S(2)}) copy-start(f32[1024,768]{0,1:T(8,128)S(1)} %get-tuple-element.324) | copy-start | bytes 9437188
  172.9 38.0 %copy-start.68 = (pred[1024]{0:T(1024)(128)(4,1)S(1)}, pred[1024]{0:T(1024)(128)(4,1)}, u32[]{:S(2)}) copy-start(pred[1024]{0:T(1024)(128)(4,1)} %broadcast_compare_fusion.2) | copy-start | bytes 3076
  254.1 339.1 %reduce-scatter.9.cloned.1.call-start = ((), (), s32[]{:S(2)}) async-start(), calls=%async_computation.10 | async-start | bytes 5898240 | tf_op jit(solution)/shard_map/reduce_scatter | solution.py:278
  263.9 329.3 %reduce-scatter.11.cloned.1.call-start = ((), (), s32[]{:S(2)}) async-start(), calls=%async_computation.11 | async-start | bytes 5898240 | tf_op jit(solution)/shard_map/reduce_scatter | solution.py:284
  288.0 352.1 %reduce-scatter.5.cloned.1.call-start = ((), (), s32[]{:S(2)}) async-start(), calls=%async_computation.8 | async-start | bytes 4423680 | tf_op jit(solution)/shard_map/reduce_scatter | solution.py:266
  307.1 18.7 %copy-start.6 = (pred[512,1024]{1,0:T(8,128)(4,1)}, pred[512,1024]{1,0:T(8,128)(4,1)S(1)}, u32[]{:S(2)}) copy-start(pred[512,1024]{1,0:T(8,128)(4,1)S(1)} %broadcast_compare_fusion.6) | copy-start | bytes 1572868 | tf_op jit(solution)/shard_map/while
  390.9 9.0 %copy-start.7 = (pred[512,1024]{1,0:T(8,128)(4,1)S(1)}, pred[512,1024]{1,0:T(8,128)(4,1)}, u32[]{:S(2)}) copy-start(pred[512,1024]{1,0:T(8,128)(4,1)} %copy-done.6) | copy-start | bytes 1572868 | tf_op jit(solution)/shard_map/while
  390.9 9.0 %copy-start.25 = (bf16[1024,12,64]{0,2,1:T(8,128)(2,1)S(1)}, bf16[1024,12,64]{0,2,1:T(8,128)(2,1)}, u32[]{:S(2)}) copy-start(bf16[1024,12,64]{0,2,1:T(8,128)(2,1)} %get-tuple-element.533) | copy-start | bytes 4718596 | tf_op jit(solution)/shard_map/while
  426.4 18.3 %copy-start.6 = (pred[512,1024]{1,0:T(8,128)(4,1)}, pred[512,1024]{1,0:T(8,128)(4,1)S(1)}, u32[]{:S(2)}) copy-start(pred[512,1024]{1,0:T(8,128)(4,1)S(1)} %broadcast_compare_fusion.6) | copy-start | bytes 1572868 | tf_op jit(solution)/shard_map/while
  507.3 9.8 %copy-start.7 = (pred[512,1024]{1,0:T(8,128)(4,1)S(1)}, pred[512,1024]{1,0:T(8,128)(4,1)}, u32[]{:S(2)}) copy-start(pred[512,1024]{1,0:T(8,128)(4,1)} %copy-done.6) | copy-start | bytes 1572868 | tf_op jit(solution)/shard_map/while
  507.3 9.8 %copy-start.25 = (bf16[1024,12,64]{0,2,1:T(8,128)(2,1)S(1)}, bf16[1024,12,64]{0,2,1:T(8,128)(2,1)}, u32[]{:S(2)}) copy-start(bf16[1024,12,64]{0,2,1:T(8,128)(2,1)} %get-tuple-element.533) | copy-start | bytes 4718596 | tf_op jit(solution)/shard_map/while
  578.2 9.0 %copy-start.14 = (bf16[1024,768]{0,1:T(8,128)(2,1)S(1)}, bf16[1024,768]{0,1:T(8,128)(2,1)}, u32[]{:S(2)}) copy-start(bf16[1024,768]{0,1:T(8,128)(2,1)} %copy-done.13) | copy-start | bytes 4718596
  578.2 9.0 %copy-start.26 = (bf16[1024,768]{1,0:T(8,128)(2,1)S(1)}, bf16[1024,768]{1,0:T(8,128)(2,1)}, u32[]{:S(2)}) copy-start(bf16[1024,768]{1,0:T(8,128)(2,1)} %copy.96) | copy-start | bytes 4718596
  578.2 9.0 %copy-start.56 = (f32[1024]{0:T(1024)S(1)}, f32[1024]{0:T(1024)}, u32[]{:S(2)}) copy-start(f32[1024]{0:T(1024)} %copy-done.55) | copy-start | bytes 12292
  578.2 9.0 %copy-start.58 = (f32[768]{0:T(1024)S(1)}, f32[768]{0:T(1024)}, u32[]{:S(2)}) copy-start(f32[768]{0:T(1024)} %copy-done.57) | copy-start | bytes 9220
  578.2 9.0 %copy-start.60 = (f32[1024]{0:T(1024)S(1)}, f32[1024]{0:T(1024)}, u32[]{:S(2)}) copy-start(f32[1024]{0:T(1024)} %copy-done.59) | copy-start | bytes 12292
  578.2 9.0 %copy-start.79 = (f32[768]{0:T(1024)S(1)}, f32[768]{0:T(1024)}, u32[]{:S(2)}) copy-start(f32[768]{0:T(1024)} %copy-done.78) | copy-start | bytes 9220
  593.1 49.6 %copy-start.95 = (bf16[192]{0:T(256)(128)(2,1)S(1)}, bf16[192]{0:T(256)(128)(2,1)}, u32[]{:S(2)}) copy-start(bf16[192]{0:T(256)(128)(2,1)} %param.31) | copy-start | bytes 1156
  593.1 124.7 %all-reduce.25.cloned.1.call-start = ((), (), s32[]{:S(2)}) async-start(), calls=%async_computation.13 | async-start | bytes 5308416 | tf_op jit(solution)/shard_map/psum | solution.py:312
  593.8 190.7 %all-gather.16.cloned.1.call-start = ((), (), s32[]{:S(2)}) async-start(), calls=%async_computation.12 | async-start | bytes 7962624 | tf_op jit(solution)/shard_map/all_gather | solution.py:10
  659.7 37.6 %copy-start.23 = (bf16[1024,768]{0,1:T(8,128)(2,1)S(1)}, bf16[1024,768]{0,1:T(8,128)(2,1)}, u32[]{:S(2)}) copy-start(bf16[1024,768]{0,1:T(8,128)(2,1)} %copy.84) | copy-start | bytes 4718596
  659.7 37.6 %copy-start.62 = (f32[1024]{0:T(1024)S(1)}, f32[1024]{0:T(1024)}, u32[]{:S(2)}) copy-start(f32[1024]{0:T(1024)} %copy-done.61) | copy-start | bytes 12292
  659.7 37.6 %copy-start.69 = (pred[1024]{0:T(1024)(128)(4,1)S(1)}, pred[1024]{0:T(1024)(128)(4,1)}, u32[]{:S(2)}) copy-start(pred[1024]{0:T(1024)(128)(4,1)} %broadcast_compare_fusion.2) | copy-start | bytes 3076
  (63 other events, 202.5 us)
Sparse Core Ops, SparseCore 0:
  9.9 50.1 all-gather.7
  62.0 27.5 all-gather.9
  91.4 56.9 all-gather.11
  150.1 56.9 all-gather.13
  254.2 28.6 reduce-scatter.6
  285.8 56.9 reduce-scatter.8
  345.8 56.9 reduce-scatter.10
  593.2 46.7 reduce-scatter.4
  642.7 69.7 all-reduce.24
  713.9 70.6 all-gather.15
